TPU v7x, 512 devices: a whole 4x8x8 slice. The times are simulated.
512 devices in a mesh: slab: 16 (over y, core), tile: 32 (over x, z).
Axes of the slice: x: 4, y: 8, z: 8, core: 2. Of those that a mesh axis runs over, the one named last changes fastest.
Arguments:
- starting_heat_state: float32 [64, 256, 2048], P('slab', 'tile'), may hold values from 0 to 2
- spot_middle_sequence: int32 [2, 2], replicated, may hold values from 0 to 2047, as said below
- crystal_label_field: int32 [128, 64, 4096], P('slab', None, 'tile'), may hold values from 0 to 4095
- growth_front_radius: float32 [128, 64, 4096], P('slab', None, 'tile'), may hold values from 0 to 1
- seed_voxel_position: int32 [32768], P(('slab', 'tile')), may hold values from 0 to 65535, as said below
- seed_crystal_label: int32 [32768], P(('slab', 'tile')), may hold values from 0 to 4095
Outputs:
- heated_state_result: float32 [64, 256, 2048], P('slab', 'tile')
- grown_envelope: float32 [128, 64, 4096], P('slab', None, 'tile')
Inputs may be any that keep to these rules, and one draw needn't show every extreme that they name: `spot_middle_sequence`: beam cells lie on the grid: the first entry below 256, the second below 2048; the last step's scan entry is 2047. `seed_voxel_position`: the sites of one device name distinct cells of its block.
All inputs are finite; a program needn't handle non-finite values.
Results may differ from a plain program's by a relative error of at most 0.00002.
Values sent between devices are 32-bit elements; how exact they have to be, the bound alone decides.
A program may use at most 64 MiB of HBM per device.

v0:
```python
import jax
import jax.numpy as jnp
from jax import lax
from jax.sharding import Mesh
from jax.sharding import PartitionSpec as P

TILE = ("tile_0", "tile_1")
SLAB_TILE = ("slab", "tile_0", "tile_1")


heat_rate = 0.1
source_power = 1.5
beam_radius_sq = 36.0
depth_scale = 3.0
liquidus = 1.0
cell_spacing = 0.5
golden_angle = 2.39996323


def padded(x, sides, width):
    for axis, dim in sides:
        peers, length = (lax.axis_size(axis), x.shape[dim])
        up = [(i, (i + 1) % peers) for i in range(peers - 1)]
        down = [(j, i) for i, j in up]
        last = lax.slice_in_dim(x, length - width, length, axis=dim)
        leading = lax.slice_in_dim(x, 0, width, axis=dim)
        before = lax.ppermute(last, axis, up)
        after = lax.ppermute(leading, axis, down)
        x = jnp.concatenate([before, x, after], axis=dim)
    return x


def in_blocks(x, dim, peers):
    shape = x.shape
    parts = x.reshape(*shape[:dim], peers, shape[dim] // peers, *shape[dim + 1 :])
    return jnp.moveaxis(parts, dim, 0)


def joined_along(parts, dim):
    parts = jnp.moveaxis(parts, 0, dim)
    shape = parts.shape
    return parts.reshape(*shape[:dim], shape[dim] * shape[dim + 1], *shape[dim + 2 :])


def moved_by_axis(parts, axes, turns):
    inside = parts.shape[1:]
    whole = parts.reshape(*(lax.axis_size(a) for a in axes), *inside)
    for k in turns:
        whole = lax.all_to_all(whole, axes[k], k, k, tiled=True)
    return whole.reshape(-1, *inside)


def exchange_by_axis(x, axes, turns, split_dim, concat_dim):
    parts = in_blocks(x, split_dim, lax.axis_size(axes))
    return joined_along(moved_by_axis(parts, axes, turns), concat_dim)


def padded_2(x, sides, width):
    edges = {}
    for axis, dim in sides:
        peers, length = (lax.axis_size(axis), x.shape[dim])
        up = [(i, (i + 1) % peers) for i in range(peers - 1)]
        last = lax.slice_in_dim(x, length - width, length, axis=dim)
        leading = lax.slice_in_dim(x, 0, width, axis=dim)
        edges[dim] = (
            lax.ppermute(last, axis, up),
            lax.ppermute(leading, axis, [(b, a) for a, b in up]),
        )
    done = []
    for _, dim in sides:
        low, high = edges[dim]
        around = [(width, width) if d in done else (0, 0) for d in range(x.ndim)]
        x = jnp.concatenate([jnp.pad(low, around), x, jnp.pad(high, around)], axis=dim)
        done.append(dim)
    return x


def conduct(field):
    square = field * field
    return 1.0 + 0.5 * square / (1.0 + square)


def march_forward(bordered_grid, z_first, x_first, beam, total_z, total_x):
    full = jnp.pad(bordered_grid, ((0, 0), (0, 0), (1, 1)))
    kfull = conduct(full)
    centre = full[1:-1, 1:-1, 1:-1]
    kcentre = kfull[1:-1, 1:-1, 1:-1]
    flux = jnp.zeros_like(centre)
    for offset in ((0, 1, 1), (2, 1, 1), (1, 0, 1), (1, 2, 1), (1, 1, 0), (1, 1, 2)):
        neigh = full[
            offset[0] : offset[0] + centre.shape[0],
            offset[1] : offset[1] + centre.shape[1],
            offset[2] : offset[2] + centre.shape[2],
        ]
        kneigh = kfull[
            offset[0] : offset[0] + centre.shape[0],
            offset[1] : offset[1] + centre.shape[1],
            offset[2] : offset[2] + centre.shape[2],
        ]
        flux = flux + 0.5 * (kcentre + kneigh) * (neigh - centre)
    zcoord = z_first + jnp.arange(centre.shape[0], dtype=jnp.int32)
    xcoord = x_first + jnp.arange(centre.shape[1], dtype=jnp.int32)
    ycoord = jnp.arange(centre.shape[2], dtype=jnp.int32)
    depth = (total_z - 1 - zcoord).astype(jnp.float32)
    xdist = (xcoord - beam[0]).astype(jnp.float32)
    ydist = (ycoord - beam[1]).astype(jnp.float32)
    plane = jnp.exp(
        -(xdist[:, None] * xdist[:, None] + ydist[None, :] * ydist[None, :]) / beam_radius_sq
    )
    source = source_power * plane[None, :, :] * jnp.exp(-depth / depth_scale)[:, None, None]
    result = centre + heat_rate * flux + source
    inside = ((zcoord >= 0) & (zcoord < total_z))[:, None, None] & (
        (xcoord >= 0) & (xcoord < total_x)
    )[None, :, None]
    return jnp.where(inside, result, jnp.zeros_like(result))


def refine_axis(bordered_grid, axis):
    count = bordered_grid.shape[axis] - 2
    before = lax.slice_in_dim(bordered_grid, 0, count, axis=axis)
    centre = lax.slice_in_dim(bordered_grid, 1, count + 1, axis=axis)
    after = lax.slice_in_dim(bordered_grid, 2, count + 2, axis=axis)
    lower = 0.25 * before + 0.75 * centre
    upper = 0.75 * centre + 0.25 * after
    stacked = jnp.stack([lower, upper], axis=axis + 1)
    array_extent = list(centre.shape)
    array_extent[axis] = 2 * count
    return stacked.reshape(array_extent)


def extend_along_dimension(field, axis):
    widths = [(0, 0), (0, 0), (0, 0)]
    widths[axis] = (1, 1)
    return jnp.pad(field, widths)


def local(
    starting_heat_state,
    spot_middle_sequence,
    crystal_label_field,
    growth_front_radius,
    seed_voxel_position,
    seed_crystal_label,
):
    slab_count = lax.axis_size("slab")
    tile_count = lax.axis_size(TILE)
    region_vertical_number, region_lateral_number, region_lengthwise_number = (
        starting_heat_state.shape
    )
    total_z = region_vertical_number * slab_count
    total_x = region_lateral_number * tile_count
    window_cells = crystal_label_field.shape[1] // 2
    window_first = (total_x - window_cells) // 2
    z_first = lax.axis_index("slab") * region_vertical_number
    x_first = lax.axis_index(TILE) * region_lateral_number
    bordered_grid = padded(starting_heat_state, (("slab", 0), (TILE, 1)), 2)
    middle = march_forward(
        bordered_grid, z_first - 1, x_first - 1, spot_middle_sequence[0], total_z, total_x
    )
    heated_state_result = march_forward(
        middle, z_first, x_first, spot_middle_sequence[1], total_z, total_x
    )
    coarse = exchange_by_axis(heated_state_result, TILE, (0, 1), 2, 1)
    broadened_grid = extend_along_dimension(coarse, 1)
    window = lax.slice_in_dim(broadened_grid, window_first, window_first + window_cells + 2, axis=1)
    edged_blocks = padded(window, (("slab", 0), (TILE, 2)), 1)
    fine_temp = refine_axis(edged_blocks, 0)
    fine_temp = refine_axis(fine_temp, 1)
    fine_temp = refine_axis(fine_temp, 2)
    nucleated = (
        crystal_label_field.reshape(-1)
        .at[seed_voxel_position]
        .set(seed_crystal_label)
        .reshape(crystal_label_field.shape)
    )
    theta = golden_angle * (nucleated % 64).astype(jnp.float32)
    speed = 1.0 + 0.5 * jnp.cos(4.0 * theta)
    under = jnp.maximum(liquidus - fine_temp, 0.0)
    grown = growth_front_radius + speed * under * under
    rim_grown = padded_2(grown, (("slab", 0), (TILE, 2)), 1)
    rim_grown = extend_along_dimension(rim_grown, 1)
    centre = rim_grown[1:-1, 1:-1, 1:-1]
    winning_choice = centre
    for offset in ((0, 1, 1), (2, 1, 1), (1, 0, 1), (1, 2, 1), (1, 1, 0), (1, 1, 2)):
        neigh = rim_grown[
            offset[0] : offset[0] + centre.shape[0],
            offset[1] : offset[1] + centre.shape[1],
            offset[2] : offset[2] + centre.shape[2],
        ]
        winning_choice = jnp.maximum(winning_choice, neigh - cell_spacing)
    return (heated_state_result, winning_choice)


def solution(mesh):
    split = Mesh(mesh.devices.reshape(mesh.shape["slab"], 4, 8), ("slab", "tile_0", "tile_1"))
    return jax.shard_map(
        local,
        mesh=split,
        in_specs=(
            P("slab", TILE, None),
            P(),
            P("slab", None, TILE),
            P("slab", None, TILE),
            P(SLAB_TILE),
            P(SLAB_TILE),
        ),
        out_specs=(P("slab", TILE, None), P("slab", None, TILE)),
        check_vma=False,
    )
```

profile of v0, /device:TPU:26, one launch (start us, length us, event | category | flops | bytes accessed | tf_op | source)
XLA Modules:
  0.0 107.1 jit_solution(17786323657157549383)
XLA Ops:
  0.6 1.0 fusion.83
  1.7 1.9 %collective-permute-start = (f32[2,8,2048]{2,1,0:T(8,128)S(1)}, f32[2,8,2048]{2,1,0:T(8,128)S(1)}, u32[]{:S(2)}, u32[]{:S(2)}) collective-permute-start(f32[2,8,2048]{2,1,0:T(8,128)S(1)} %get-tuple-element.15), channel_id=1, source_target_pairs={{0,32},{32,64},{64,96},{96,128},{128,160},{160,192},{192,224},{224... | collective-permute-start | bytes 393224 | tf_op jit(solution)/shard_map/ppermute | solution.py:27
  3.6 3.6 %collective-permute-start.1 = (f32[2,8,2048]{2,1,0:T(8,128)S(1)}, f32[2,8,2048]{2,1,0:T(8,128)S(1)}, u32[]{:S(2)}, u32[]{:S(2)}) collective-permute-start(f32[2,8,2048]{2,1,0:T(8,128)S(1)} %get-tuple-element.14), channel_id=1, source_target_pairs={{32,0},{64,32},{96,64},{128,96},{160,128},{192,160},{224,192},{256... | collective-permute-start | bytes 393224 | tf_op jit(solution)/shard_map/ppermute | solution.py:28
  7.3 1.4 %fusion.85 = (s32[1,1]{1,0:T(1,128)}, s32[1,1]{1,0:T(1,128)}, s32[1,1]{1,0:T(1,128)}, s32[1,1]{1,0:T(1,128)}) fusion(s32[2,2]{1,0:T(2,128)} %param.7), kind=kLoop, calls=%fused_computation.169 | loop fusion | bytes 32 | tf_op jit(solution)/shard_map/slice | solution.py:105
  8.7 0.6 convert_multiply_fusion.3
  9.3 0.7 convert_multiply_fusion.1
  10.0 0.7 convert_multiply_fusion.2
  10.6 0.6 convert_multiply_fusion
  11.8 4.3 %collective-permute-start.2 = (f32[8,2,2048]{2,1,0:T(2,128)S(1)}, f32[8,2,2048]{2,1,0:T(2,128)S(1)}, u32[]{:S(2)}, u32[]{:S(2)}) collective-permute-start(f32[8,2,2048]{2,1,0:T(2,128)S(1)} %get-tuple-element.6), channel_id=1, source_target_pairs={{0,1},{1,2},{2,3},{3,4},{4,5},{5,6},{6,7},{7,8},{8,9},{9,10},{10,1... | collective-permute-start | bytes 393224 | tf_op jit(solution)/shard_map/ppermute | solution.py:27
  16.1 8.6 %collective-permute-start.3 = (f32[8,2,2048]{2,1,0:T(2,128)S(1)}, f32[8,2,2048]{2,1,0:T(2,128)S(1)}, u32[]{:S(2)}, u32[]{:S(2)}) collective-permute-start(f32[8,2,2048]{2,1,0:T(2,128)S(1)} %get-tuple-element.7), channel_id=1, source_target_pairs={{1,0},{2,1},{3,2},{4,3},{5,4},{6,5},{7,6},{8,7},{9,8},{10,9},{11,1... | collective-permute-start | bytes 393224 | tf_op jit(solution)/shard_map/ppermute | solution.py:28
  24.7 1.0 collective-permute-done.2
  25.7 1.5 %collective-permute-done.3 = f32[8,2,2048]{2,1,0:T(2,128)S(1)} collective-permute-done((f32[8,2,2048]{2,1,0:T(2,128)S(1)}, f32[8,2,2048]{2,1,0:T(2,128)S(1)}, u32[]{:S(2)}, u32[]{:S(2)}) %collective-permute-start.3) | collective-permute-done | bytes 131104 | tf_op jit(solution)/shard_map/ppermute | solution.py:28
  27.2 0.2 pad_maximum_fusion
  27.3 0.4 divide_add_fusion
  27.7 1.9 %fusion.7 = f32[6,10,2048]{2,1,0:T(8,128)S(1)} fusion(f32[8,12,2048]{2,1,0:T(8,128)S(1)} %pad_maximum_fusion, f32[8,12,2050]{2,1,0:T(8,128)S(1)} %divide_add_fusion, f32[8,2,2048]{2,1,0:T(2,128)S(1)} %collective-permute-done.3, f32[8,8,2048]{2,1,0:T(8,128)S(1)} %constant_dynamic-update-slice_fusion, f32[8,2,2048]{2,1,0:T(2,128)S(1)} %collective-permute-done.2, ...), kind=kLoop, calls=%fused_computation.15 | loop fusion | flops 4423680 | bytes 10323456 | tf_op jit(solution)/shard_map/jit(_where)/select_n | solution.py:115
  29.7 0.3 divide_add_fusion.1
  30.0 0.7 fusion.41
  30.6 0.2 reshape.243
  30.9 0.3 reshape.258
  31.3 11.0 %all_to_all.10 = f32[4,1,16384]{2,1,0:T(1,128)S(1)} all-to-all(f32[4,1,16384]{2,1,0:T(1,128)S(1)} %reshape.258), channel_id=1, replica_groups=mesh['slab'=16,'tile_0'=4,'tile_1'=8] {'tile_0'}, dimensions={0} | all-to-all | bytes 524288 | tf_op jit(solution)/shard_map/all_to_all | solution.py:49
  42.4 0.5 broadcast.377
  42.9 1.4 %reduce = f32[4,16384]{1,0:T(4,128)S(1)} reduce(f32[4,1,16384]{2,1,0:T(1,128)S(1)} %all_to_all.10, f32[]{:T(128)} %broadcast.377), dimensions={1}, to_apply=%all_to_all.6.reduce_sub_computation | reduce | bytes 524292 | tf_op jit(solution)/shard_map/all_to_all | solution.py:49
  44.2 0.3 reshape.259
  44.5 0.3 copy.74
  44.9 0.5 reshape.260
  45.4 17.9 %all_to_all.11 = f32[8,1,8192]{2,1,0:T(1,128)S(1)} all-to-all(f32[8,1,8192]{2,1,0:T(1,128)S(1)} %reshape.260), channel_id=1, replica_groups=mesh['slab'=16,'tile_0'=4,'tile_1'=8] {'tile_1'}, dimensions={0} | all-to-all | bytes 524288 | tf_op jit(solution)/shard_map/all_to_all | solution.py:49
  63.3 1.3 %reduce.1 = f32[8,8192]{1,0:T(8,128)S(1)} reduce(f32[8,1,8192]{2,1,0:T(1,128)S(1)} %all_to_all.11, f32[]{:T(128)} %broadcast.377), dimensions={1}, to_apply=%all_to_all.7.reduce_sub_computation | reduce | bytes 524292 | tf_op jit(solution)/shard_map/all_to_all | solution.py:49
  64.5 0.3 reshape.261
  65.0 1.9 %collective-permute-start.4 = (f32[1,34,64]{2,1,0:T(8,128)S(1)}, f32[1,34,64]{2,1,0:T(8,128)S(1)}, u32[]{:S(2)}, u32[]{:S(2)}) collective-permute-start(f32[1,34,64]{2,1,0:T(8,128)S(1)} %get-tuple-element.4), channel_id=1, source_target_pairs={{0,32},{32,64},{64,96},{96,128},{128,160},{160,192},{192,224},{224... | collective-permute-start | bytes 26120 | tf_op jit(solution)/shard_map/ppermute | solution.py:27
  66.9 3.6 %collective-permute-start.5 = (f32[1,34,64]{2,1,0:T(8,128)S(1)}, f32[1,34,64]{2,1,0:T(8,128)S(1)}, u32[]{:S(2)}, u32[]{:S(2)}) collective-permute-start(f32[1,34,64]{2,1,0:T(8,128)S(1)} %get-tuple-element.5), channel_id=1, source_target_pairs={{32,0},{64,32},{96,64},{128,96},{160,128},{192,160},{224,192},{256... | collective-permute-start | bytes 26120 | tf_op jit(solution)/shard_map/ppermute | solution.py:28
  70.6 1.4 %collective-permute-done.5 = f32[1,34,64]{2,1,0:T(8,128)S(1)} collective-permute-done((f32[1,34,64]{2,1,0:T(8,128)S(1)}, f32[1,34,64]{2,1,0:T(8,128)S(1)}, u32[]{:S(2)}, u32[]{:S(2)}) %collective-permute-start.5) | collective-permute-done | bytes 8736 | tf_op jit(solution)/shard_map/ppermute | solution.py:28
  72.1 2.5 %collective-permute-start.6 = (f32[6,34,1]{2,1,0:T(8,128)S(1)}, f32[6,34,1]{2,1,0:T(8,128)S(1)}, u32[]{:S(2)}, u32[]{:S(2)}) collective-permute-start(f32[6,34,1]{2,1,0:T(8,128)S(1)} %get-tuple-element.20), channel_id=1, source_target_pairs={{0,1},{1,2},{2,3},{3,4},{4,5},{5,6},{6,7},{7,8},{8,9},{9,10},{10,1... | collective-permute-start | bytes 2456 | tf_op jit(solution)/shard_map/ppermute | solution.py:27
  74.6 5.5 %collective-permute-start.7 = (f32[6,34,1]{2,1,0:T(8,128)S(1)}, f32[6,34,1]{2,1,0:T(8,128)S(1)}, u32[]{:S(2)}, u32[]{:S(2)}) collective-permute-start(f32[6,34,1]{2,1,0:T(8,128)S(1)} %get-tuple-element.21), channel_id=1, source_target_pairs={{1,0},{2,1},{3,2},{4,3},{5,4},{6,5},{7,6},{8,7},{9,8},{10,9},{11,1... | collective-permute-start | bytes 2456 | tf_op jit(solution)/shard_map/ppermute | solution.py:28
  80.2 0.9 scatter_fusion
  81.1 1.6 %collective-permute-done.7 = f32[6,34,1]{2,1,0:T(8,128)S(1)} collective-permute-done((f32[6,34,1]{2,1,0:T(8,128)S(1)}, f32[6,34,1]{2,1,0:T(8,128)S(1)}, u32[]{:S(2)}, u32[]{:S(2)}) %collective-permute-start.7) | collective-permute-done | bytes 848 | tf_op jit(solution)/shard_map/ppermute | solution.py:28
  83.1 0.2 fusion.57
  83.4 0.3 copy.65
  83.7 0.2 copy.66
  83.9 0.4 copy-done.3
  84.3 1.0 fusion.33
  85.3 3.1 %collective-permute-start.8 = (f32[1,64,128]{2,1,0:T(8,128)S(1)}, f32[1,64,128]{2,1,0:T(8,128)S(1)}, u32[]{:S(2)}, u32[]{:S(2)}) collective-permute-start(f32[1,64,128]{2,1,0:T(8,128)S(1)} %get-tuple-element.10), channel_id=1, source_target_pairs={{0,32},{32,64},{64,96},{96,128},{128,160},{160,192},{192,224},{224... | collective-permute-start | bytes 98312 | tf_op jit(solution)/shard_map/ppermute | solution.py:66
  88.5 2.4 %collective-permute-start.9 = (f32[1,64,128]{2,1,0:T(8,128)S(1)}, f32[1,64,128]{2,1,0:T(8,128)S(1)}, u32[]{:S(2)}, u32[]{:S(2)}) collective-permute-start(f32[1,64,128]{2,1,0:T(8,128)S(1)} %get-tuple-element.11), channel_id=1, source_target_pairs={{32,0},{64,32},{96,64},{128,96},{160,128},{192,160},{224,192},{256... | collective-permute-start | bytes 98312 | tf_op jit(solution)/shard_map/ppermute | solution.py:67
  91.0 1.9 %collective-permute-start.10 = (f32[8,64,1]{2,1,0:T(8,128)S(1)}, f32[8,64,1]{2,1,0:T(8,128)S(1)}, u32[]{:S(2)}, u32[]{:S(2)}) collective-permute-start(f32[8,64,1]{2,1,0:T(8,128)S(1)} %get-tuple-element.8), channel_id=1, source_target_pairs={{0,1},{1,2},{2,3},{3,4},{4,5},{5,6},{6,7},{7,8},{8,9},{9,10},{10,1... | collective-permute-start | bytes 6152 | tf_op jit(solution)/shard_map/ppermute | solution.py:66
  93.0 6.5 %collective-permute-start.11 = (f32[8,64,1]{2,1,0:T(8,128)S(1)}, f32[8,64,1]{2,1,0:T(8,128)S(1)}, u32[]{:S(2)}, u32[]{:S(2)}) collective-permute-start(f32[8,64,1]{2,1,0:T(8,128)S(1)} %get-tuple-element.9), channel_id=1, source_target_pairs={{1,0},{2,1},{3,2},{4,3},{5,4},{6,5},{7,6},{8,7},{9,8},{10,9},{11,1... | collective-permute-start | bytes 6152 | tf_op jit(solution)/shard_map/ppermute | solution.py:67
  99.5 4.9 %collective-permute-done.10 = f32[8,64,1]{2,1,0:T(8,128)S(1)} collective-permute-done((f32[8,64,1]{2,1,0:T(8,128)S(1)}, f32[8,64,1]{2,1,0:T(8,128)S(1)}, u32[]{:S(2)}, u32[]{:S(2)}) %collective-permute-start.10) | collective-permute-done | bytes 2080 | tf_op jit(solution)/shard_map/ppermute | solution.py:66
  104.5 1.2 %collective-permute-done.11 = f32[8,64,1]{2,1,0:T(8,128)S(1)} collective-permute-done((f32[8,64,1]{2,1,0:T(8,128)S(1)}, f32[8,64,1]{2,1,0:T(8,128)S(1)}, u32[]{:S(2)}, u32[]{:S(2)}) %collective-permute-start.11) | collective-permute-done | bytes 2080 | tf_op jit(solution)/shard_map/ppermute | solution.py:67
  105.7 0.4 select_maximum_fusion
  106.0 1.1 %fusion.45 = f32[8,64,128]{2,1,0:T(8,128)} fusion(f32[10,64,1]{2,1,0:T(8,128)S(1)} %pad.24, f32[1,64,128]{2,1,0:T(8,128)S(1)} %collective-permute-done.9, f32[8,64,128]{2,1,0:T(8,128)S(1)} %fusion.33, f32[1,64,128]{2,1,0:T(8,128)S(1)} %collective-permute-done.8, f32[10,64,1]{2,1,0:T(8,128)S(1)} %pad.23, f32[10,66,130]{2,1,0:T(8,128)S(1)} %select_maximum_fusion), kind=kLoop, calls=%fused_computation.75 | loop fusion | flops 1310720 | bytes 1119232 | tf_op jit(solution)/shard_map/max | solution.py:190
  (50 shorter events, 1.4 us)
Async XLA Ops:
  0.6 11.0 %copy-start.2 = (f32[4,8,2048]{2,1,0:T(8,128)S(1)}, f32[4,8,2048]{2,1,0:T(8,128)}, u32[]{:S(2)}) copy-start(f32[4,8,2048]{2,1,0:T(8,128)} %param.6) | copy-start | bytes 786436
  1.7 9.9 %collective-permute-start = (f32[2,8,2048]{2,1,0:T(8,128)S(1)}, f32[2,8,2048]{2,1,0:T(8,128)S(1)}, u32[]{:S(2)}, u32[]{:S(2)}) collective-permute-start(f32[2,8,2048]{2,1,0:T(8,128)S(1)} %get-tuple-element.15), channel_id=1, source_target_pairs={{0,32},{32,64},{64,96},{96,128},{128,160},{160,192},{192,224},{224... | collective-permute-start | bytes 393224 | tf_op jit(solution)/shard_map/ppermute | solution.py:27
  3.6 8.1 %collective-permute-start.1 = (f32[2,8,2048]{2,1,0:T(8,128)S(1)}, f32[2,8,2048]{2,1,0:T(8,128)S(1)}, u32[]{:S(2)}, u32[]{:S(2)}) collective-permute-start(f32[2,8,2048]{2,1,0:T(8,128)S(1)} %get-tuple-element.14), channel_id=1, source_target_pairs={{32,0},{64,32},{96,64},{128,96},{160,128},{192,160},{224,192},{256... | collective-permute-start | bytes 393224 | tf_op jit(solution)/shard_map/ppermute | solution.py:28
  11.8 13.9 %collective-permute-start.2 = (f32[8,2,2048]{2,1,0:T(2,128)S(1)}, f32[8,2,2048]{2,1,0:T(2,128)S(1)}, u32[]{:S(2)}, u32[]{:S(2)}) collective-permute-start(f32[8,2,2048]{2,1,0:T(2,128)S(1)} %get-tuple-element.6), channel_id=1, source_target_pairs={{0,1},{1,2},{2,3},{3,4},{4,5},{5,6},{6,7},{7,8},{8,9},{9,10},{10,1... | collective-permute-start | bytes 393224 | tf_op jit(solution)/shard_map/ppermute | solution.py:27
  16.1 11.1 %collective-permute-start.3 = (f32[8,2,2048]{2,1,0:T(2,128)S(1)}, f32[8,2,2048]{2,1,0:T(2,128)S(1)}, u32[]{:S(2)}, u32[]{:S(2)}) collective-permute-start(f32[8,2,2048]{2,1,0:T(2,128)S(1)} %get-tuple-element.7), channel_id=1, source_target_pairs={{1,0},{2,1},{3,2},{4,3},{5,4},{6,5},{7,6},{8,7},{9,8},{10,9},{11,1... | collective-permute-start | bytes 393224 | tf_op jit(solution)/shard_map/ppermute | solution.py:28
  30.6 0.7 copy-start.1
  64.9 15.2 %copy-start.5 = (s32[64]{0:T(128)S(1)}, s32[64]{0:T(128)}, u32[]{:S(2)}) copy-start(s32[64]{0:T(128)} %param.10) | copy-start | bytes 772
  64.9 15.2 %copy-start = (s32[8,64,128]{2,1,0:T(8,128)S(1)}, s32[8,64,128]{2,1,0:T(8,128)}, u32[]{:S(2)}) copy-start(s32[8,64,128]{2,1,0:T(8,128)} %param.8) | copy-start | bytes 786436
  64.9 15.2 %copy-start.4 = (s32[64]{0:T(128)S(1)}, s32[64]{0:T(128)}, u32[]{:S(2)}) copy-start(s32[64]{0:T(128)} %param.11) | copy-start | bytes 772
  65.0 5.6 %collective-permute-start.4 = (f32[1,34,64]{2,1,0:T(8,128)S(1)}, f32[1,34,64]{2,1,0:T(8,128)S(1)}, u32[]{:S(2)}, u32[]{:S(2)}) collective-permute-start(f32[1,34,64]{2,1,0:T(8,128)S(1)} %get-tuple-element.4), channel_id=1, source_target_pairs={{0,32},{32,64},{64,96},{96,128},{128,160},{160,192},{192,224},{224... | collective-permute-start | bytes 26120 | tf_op jit(solution)/shard_map/ppermute | solution.py:27
  66.9 5.1 %collective-permute-start.5 = (f32[1,34,64]{2,1,0:T(8,128)S(1)}, f32[1,34,64]{2,1,0:T(8,128)S(1)}, u32[]{:S(2)}, u32[]{:S(2)}) collective-permute-start(f32[1,34,64]{2,1,0:T(8,128)S(1)} %get-tuple-element.5), channel_id=1, source_target_pairs={{32,0},{64,32},{96,64},{128,96},{160,128},{192,160},{224,192},{256... | collective-permute-start | bytes 26120 | tf_op jit(solution)/shard_map/ppermute | solution.py:28
  72.1 9.0 %collective-permute-start.6 = (f32[6,34,1]{2,1,0:T(8,128)S(1)}, f32[6,34,1]{2,1,0:T(8,128)S(1)}, u32[]{:S(2)}, u32[]{:S(2)}) collective-permute-start(f32[6,34,1]{2,1,0:T(8,128)S(1)} %get-tuple-element.20), channel_id=1, source_target_pairs={{0,1},{1,2},{2,3},{3,4},{4,5},{5,6},{6,7},{7,8},{8,9},{9,10},{10,1... | collective-permute-start | bytes 2456 | tf_op jit(solution)/shard_map/ppermute | solution.py:27
  74.6 8.1 %collective-permute-start.7 = (f32[6,34,1]{2,1,0:T(8,128)S(1)}, f32[6,34,1]{2,1,0:T(8,128)S(1)}, u32[]{:S(2)}, u32[]{:S(2)}) collective-permute-start(f32[6,34,1]{2,1,0:T(8,128)S(1)} %get-tuple-element.21), channel_id=1, source_target_pairs={{1,0},{2,1},{3,2},{4,3},{5,4},{6,5},{7,6},{8,7},{9,8},{10,9},{11,1... | collective-permute-start | bytes 2456 | tf_op jit(solution)/shard_map/ppermute | solution.py:28
  83.4 1.0 copy-start.3
  85.3 20.3 %collective-permute-start.8 = (f32[1,64,128]{2,1,0:T(8,128)S(1)}, f32[1,64,128]{2,1,0:T(8,128)S(1)}, u32[]{:S(2)}, u32[]{:S(2)}) collective-permute-start(f32[1,64,128]{2,1,0:T(8,128)S(1)} %get-tuple-element.10), channel_id=1, source_target_pairs={{0,32},{32,64},{64,96},{96,128},{128,160},{160,192},{192,224},{224... | collective-permute-start | bytes 98312 | tf_op jit(solution)/shard_map/ppermute | solution.py:66
  88.5 17.2 %collective-permute-start.9 = (f32[1,64,128]{2,1,0:T(8,128)S(1)}, f32[1,64,128]{2,1,0:T(8,128)S(1)}, u32[]{:S(2)}, u32[]{:S(2)}) collective-permute-start(f32[1,64,128]{2,1,0:T(8,128)S(1)} %get-tuple-element.11), channel_id=1, source_target_pairs={{32,0},{64,32},{96,64},{128,96},{160,128},{192,160},{224,192},{256... | collective-permute-start | bytes 98312 | tf_op jit(solution)/shard_map/ppermute | solution.py:67
  91.0 13.4 %collective-permute-start.10 = (f32[8,64,1]{2,1,0:T(8,128)S(1)}, f32[8,64,1]{2,1,0:T(8,128)S(1)}, u32[]{:S(2)}, u32[]{:S(2)}) collective-permute-start(f32[8,64,1]{2,1,0:T(8,128)S(1)} %get-tuple-element.8), channel_id=1, source_target_pairs={{0,1},{1,2},{2,3},{3,4},{4,5},{5,6},{6,7},{7,8},{8,9},{9,10},{10,1... | collective-permute-start | bytes 6152 | tf_op jit(solution)/shard_map/ppermute | solution.py:66
  93.0 12.6 %collective-permute-start.11 = (f32[8,64,1]{2,1,0:T(8,128)S(1)}, f32[8,64,1]{2,1,0:T(8,128)S(1)}, u32[]{:S(2)}, u32[]{:S(2)}) collective-permute-start(f32[8,64,1]{2,1,0:T(8,128)S(1)} %get-tuple-element.9), channel_id=1, source_target_pairs={{1,0},{2,1},{3,2},{4,3},{5,4},{6,5},{7,6},{8,7},{9,8},{10,9},{11,1... | collective-permute-start | bytes 6152 | tf_op jit(solution)/shard_map/ppermute | solution.py:67
where the time goes:
time: 108 us; the launch traced here: 107 us
  starting transfers between devices  45.9 us (42%)
  blocking collectives  28.9 us (27%)
  other arithmetic  11.9 us (11%)
  waiting for transfers between devices  11.6 us (11%)
  local copies, waits for them, and re-layouts  7.6 us (7%)
  between operations  1.2 us (1%)
    all_to_all x2, blocking collectives, moved_by_axis(): whole = lax.all_to_all(whole, axes[k], k, k, tiled=True)  28.9 us
    ppermute x4, starting transfers between devices, padded(): after = lax.ppermute(leading, axis, down)  21.3 us
    ppermute x4, starting transfers between devices, padded(): before = lax.ppermute(last, axis, up)  10.6 us
    ppermute x2, starting transfers between devices, padded_2(): lax.ppermute(leading, axis, [(b, a) for a, b in up])  8.93 us
    ppermute x2, starting transfers between devices, padded_2(): lax.ppermute(last, axis, up)  5.05 us
    ppermute x2, waiting for transfers between devices, padded_2(): lax.ppermute(last, axis, up)  4.95 us
    ppermute x4, waiting for transfers between devices, padded(): after = lax.ppermute(leading, axis, down)  4.53 us
    all_to_all x2, other arithmetic, moved_by_axis(): whole = lax.all_to_all(whole, axes[k], k, k, tiled=True)  2.63 us
  transfers between devices with their start and end apart: 12, of which 6 were waited for; matrix products, arithmetic and copies ran while one was open for 5% of the time, Pallas kernels for 0%

commit v1 on v0

v1 whole, which is shorter than its diff:
```python
import jax
import jax.numpy as jnp
from jax import lax
from jax.experimental import pallas as pl
from jax.experimental.pallas import tpu as pltpu
from jax.sharding import PartitionSpec as P

HEAT_RATE = 0.1
SOURCE_POWER = 1.5
BEAM_RADIUS_SQ = 36.0
DEPTH_SCALE = 3.0
GOLDEN_ANGLE = 2.39996323
MESH = pl.DeviceIdType.MESH
F32 = jnp.float32
NEIGHBOURS = [(a, b) for a in (-1, 0, 1) for b in (-1, 0, 1) if (a, b) != (0, 0)]


def lanes(rows):
    return lax.broadcasted_iota(jnp.int32, (rows, 128), 1)


def lane_pick(x, index):
    return jnp.take_along_axis(x, index, axis=1)


def conductance(v):
    return 0.5 * HEAT_RATE * 1.5 - (0.25 * HEAT_RATE) / (1.0 + v * v)


def next_along_y(x, last):
    r = pltpu.roll(x, 127, 2)
    up = pltpu.roll(r, 15, 1)
    lane = lax.broadcasted_iota(jnp.int32, x.shape, 2)
    row = lax.broadcasted_iota(jnp.int32, x.shape, 1)
    up = jnp.where(row == 15, last, up)
    return jnp.where(lane == 127, up, r)


def before_along_y(x, first):
    r = pltpu.roll(x, 1, 2)
    down = pltpu.roll(r, 1, 1)
    lane = lax.broadcasted_iota(jnp.int32, x.shape, 2)
    row = lax.broadcasted_iota(jnp.int32, x.shape, 1)
    down = jnp.where(row == 0, first, down)
    return jnp.where(lane == 0, down, r)


def heat_step(src, cond, dst, plane, depth, count_z, count_x, offset_x):
    def conductances(z, c):
        cond[z] = conductance(src[z])
        return c

    lax.fori_loop(0, count_z, conductances, 0)

    def layer(z, c):
        v = src[z + 1]
        p = cond[z + 1]
        flux_x = (p[:-1] + p[1:]) * (v[1:] - v[:-1])
        inner = slice(1, count_x - 1)
        vc, pc = v[inner], p[inner]
        total = flux_x[1:] - flux_x[:-1]
        total += (pc + cond[z, 1 : count_x - 1]) * (src[z, 1 : count_x - 1] - vc)
        total += (pc + cond[z + 2, 1 : count_x - 1]) * (src[z + 2, 1 : count_x - 1] - vc)
        outside = 0.5 * HEAT_RATE
        flux_y = (pc + next_along_y(pc, outside)) * (next_along_y(vc, 0.0) - vc)
        edge = (pc + outside) * vc
        low = jnp.broadcast_to(edge[:, 0:1, 0:1], vc.shape)
        total += flux_y - before_along_y(flux_y, low)
        source = plane[offset_x : offset_x + count_x - 2] * depth[z]
        dst[z] = vc + total + source
        return c

    lax.fori_loop(0, count_z - 2, layer, 0)


def kernel(
    n_slab,
    n_tile,
    x_in,
    spot_in,
    lab_in,
    rad_in,
    pos_in,
    seed_in,
    heat_out,
    grown_out,
    x_v,
    spot,
    lab,
    rad,
    pos,
    seed,
    spd,
    E,
    PE,
    M,
    H,
    plane,
    depth,
    pk,
    hrow,
    ek,
    W,
    Ph,
    Pe,
    X,
    face_rad,
    face_spd,
    cols,
    col_in,
    side_rad,
    side_spd,
    Gf,
    env,
    in_sem,
    out_sem,
    send_a,
    recv_a,
    send_b,
    recv_b,
    ready,
):
    s = lax.axis_index("slab")
    t = lax.axis_index("tile")
    main = tuple(range(n_tile // 2 - 2, n_tile // 2 + 2))
    edges = (main[0] - 1, main[-1] + 1)
    sources = (edges[0],) + main + (edges[1],)
    is_main = (t >= main[0]) & (t <= main[-1])
    is_source = (t >= sources[0]) & (t <= sources[-1])
    is_edge = is_source & jnp.logical_not(is_main)

    def there(a, b):
        c = jnp.bool_(True)
        if a == -1:
            c = c & (s > 0)
        if a == 1:
            c = c & (s < n_slab - 1)
        if b == -1:
            c = c & (t > 0)
        if b == 1:
            c = c & (t < n_tile - 1)
        return c

    bar = pltpu.get_barrier_semaphore()
    count = jnp.int32(0)
    for a, b in NEIGHBOURS:
        c = there(a, b)

        @pl.when(c)
        def _():
            pl.semaphore_signal(bar, inc=1, device_id=(s + a, t + b), device_id_type=MESH)

        count = count + c.astype(jnp.int32)

    @pl.when(is_source)
    def _():
        @pl.loop(0, n_tile)
        def _(d):
            @pl.when(d != t)
            def _():
                pl.semaphore_signal(bar, inc=1, device_id=(s, d), device_id_type=MESH)

    count = count + len(sources) - is_source.astype(jnp.int32)

    loads = [
        pltpu.make_async_copy(a, b, in_sem.at[i])
        for i, (a, b) in enumerate(
            (
                (x_in, x_v),
                (lab_in, lab),
                (rad_in, rad),
                (spot_in, spot),
                (pos_in, pos),
                (seed_in, seed),
            )
        )
    ]
    for c in loads:
        c.start()

    @pl.when(s == 0)
    def _():
        E[0:3] = jnp.zeros((3,) + E.shape[1:], F32)

    @pl.when(s == n_slab - 1)
    def _():
        E[7:10] = jnp.zeros((3,) + E.shape[1:], F32)

    @pl.when(t == 0)
    def _():
        E[:, 0:2] = jnp.zeros((10, 2) + E.shape[2:], F32)
        col_in[0] = jnp.zeros(col_in.shape[1:], F32)

    @pl.when(t == n_tile - 1)
    def _():
        E[:, 10:12] = jnp.zeros((10, 2) + E.shape[2:], F32)
        col_in[1] = jnp.zeros(col_in.shape[1:], F32)

    @pl.when(s == 0)
    def _():
        face_rad[0] = jnp.zeros((64, 128), F32)
        face_spd[0] = jnp.zeros((64, 128), F32)

    @pl.when(s == n_slab - 1)
    def _():
        face_rad[1] = jnp.zeros((64, 128), F32)
        face_spd[1] = jnp.zeros((64, 128), F32)

    loads[0].wait()
    flat = E.reshape(10 * 12 * 16, 128)
    for z in range(4):
        for k in range(16):
            row = ((z + 3) * 12 + 2) * 16 + k
            flat[pl.ds(row, 8, stride=16), :] = x_v[z, :, 128 * k : 128 * k + 128]

    pl.semaphore_wait(bar, count)

    halos = []
    for a, b in NEIGHBOURS:
        zs = {0: (3, 4, 3), -1: (3, 3, 7), 1: (4, 3, 0)}[a]
        xs = {0: (2, 8, 2), -1: (2, 2, 10), 1: (8, 2, 0)}[b]
        if a != 0 and b != 0:
            zs = {-1: (3, 2, 7), 1: (5, 2, 1)}[a]
        k = len(halos)
        halos.append(
            (
                a,
                b,
                pltpu.make_async_remote_copy(
                    src_ref=E.at[pl.ds(zs[0], zs[1]), pl.ds(xs[0], xs[1])],
                    dst_ref=E.at[pl.ds(zs[2], zs[1]), pl.ds(xs[2], xs[1])],
                    send_sem=send_a.at[k],
                    recv_sem=recv_a.at[k],
                    device_id=(s + a, t + b),
                    device_id_type=MESH,
                ),
            )
        )
    for a, b, copy in halos:

        @pl.when(there(a, b))
        def _():
            copy.start()

    for q in sources:

        @pl.when(t != q)
        def _():
            pl.semaphore_signal(ready, inc=1, device_id=(s, jnp.int32(q)), device_id_type=MESH)

    for c in loads[1:]:
        c.wait()
    place = pos[...].reshape(1, 64)
    value = ((seed[...].reshape(1, 64) & 63) + 1).astype(F32)
    rows = lax.broadcasted_iota(jnp.int32, (512, 64), 0)
    cells = lax.broadcasted_iota(jnp.int32, (128, 64), 0)
    in_row = jnp.where(rows == (place >> 7), 1.0, 0.0).astype(jnp.bfloat16)
    in_lane = jnp.where(cells == (place & 127), value, 0.0).astype(jnp.bfloat16)
    named = lax.dot_general(
        in_row, in_lane, (((1,), (1,)), ((), ())), preferred_element_type=F32
    ).reshape(8, 64, 128)
    theta = GOLDEN_ANGLE * lanes(8).astype(F32)
    table = 1.0 + 0.5 * jnp.cos(4.0 * theta)
    table = jnp.broadcast_to(table[0:1], (64, 128))
    for z in range(8):
        grain = jnp.where(named[z] > 0.5, named[z].astype(jnp.int32) - 1, lab[z] & 63)
        spd[z] = lane_pick(table, grain)

    pick_r = lax.broadcasted_iota(jnp.int32, (8, 128), 0)
    lane8 = lanes(8)
    nt = (((1,), (1,)), ((), ()))
    e_rad = jnp.where(
        ((pick_r == 0) & (lane8 == 127)) | ((pick_r == 2) & (lane8 == 0)), 1.0, 0.0
    )
    e_spd = jnp.where(
        ((pick_r == 1) & (lane8 == 127)) | ((pick_r == 3) & (lane8 == 0)), 1.0, 0.0
    )
    hi = lax.Precision.HIGHEST
    cols[...] = lax.dot_general(
        e_rad, rad[...].reshape(512, 128), nt, precision=hi, preferred_element_type=F32
    ) + lax.dot_general(
        e_spd, spd[...].reshape(512, 128), nt, precision=hi, preferred_element_type=F32
    )

    for step in range(2):
        row = lax.broadcasted_iota(jnp.int32, (12, 16, 128), 0)
        y = lax.broadcasted_iota(jnp.int32, (12, 16, 128), 1) * 128
        y = y + lax.broadcasted_iota(jnp.int32, (12, 16, 128), 2)
        xd = (t * 8 - 2 + row - spot[step, 0]).astype(F32)
        yd = (y - spot[step, 1]).astype(F32)
        plane[step] = SOURCE_POWER * jnp.exp(-(xd * xd + yd * yd) / BEAM_RADIUS_SQ)
    level = lax.broadcasted_iota(jnp.int32, (8, 16, 128), 0) + (s * 4 - 2)
    depth[...] = jnp.exp(-(n_slab * 4 - 1 - level).astype(F32) / DEPTH_SCALE)

    fine = []
    k0 = len(NEIGHBOURS)
    for a, z in ((1, 7), (-1, 0)):
        slot = 0 if a == 1 else 1
        fine.append((a, 0, rad.at[z], face_rad.at[slot], (s + a, t)))
        fine.append((a, 0, spd.at[z], face_spd.at[slot], (s + a, t)))
    for b in (1, -1):
        slot = 0 if b == 1 else 1
        fine.append((0, b, cols, col_in.at[slot], (s, t + b)))
    fine = [
        (
            a,
            b,
            pltpu.make_async_remote_copy(
                src_ref=src,
                dst_ref=dst,
                send_sem=send_a.at[k0 + i],
                recv_sem=recv_a.at[k0 + i],
                device_id=to,
                device_id_type=MESH,
            ),
        )
        for i, (a, b, src, dst, to) in enumerate(fine)
    ]
    for a, b, copy in fine:

        @pl.when(there(a, b))
        def _():
            copy.start()

    for a, b, copy in halos:

        @pl.when(there(-a, -b))
        def _():
            copy.wait_recv()

    for a, b, copy in halos:

        @pl.when(there(a, b))
        def _():
            copy.wait_send()

    heat_step(E, PE, M, plane.at[0], depth, 10, 12, 1)

    @pl.when(s == 0)
    def _():
        M[0:2] = jnp.zeros((2,) + M.shape[1:], F32)

    @pl.when(s == n_slab - 1)
    def _():
        M[6:8] = jnp.zeros((2,) + M.shape[1:], F32)

    @pl.when(t == 0)
    def _():
        M[:, 0:1] = jnp.zeros((8, 1) + M.shape[2:], F32)

    @pl.when(t == n_tile - 1)
    def _():
        M[:, 9:10] = jnp.zeros((8, 1) + M.shape[2:], F32)

    heat_step(M, PE.at[0:8, 0:10], H, plane.at[1], depth.at[1:7], 8, 10, 2)

    @pl.when(s == 0)
    def _():
        H[0] = jnp.zeros(H.shape[1:], F32)

    @pl.when(s == n_slab - 1)
    def _():
        H[5] = jnp.zeros(H.shape[1:], F32)

    Hf = H.reshape(6 * 8 * 16, 128)

    def cut(read, n):
        lane = lanes(n)

        def pieces(k):
            now = [read(z, k) for z in range(6)]
            low = [jnp.where(k > 0, read(z, jnp.maximum(k - 1, 0)), 0.0) for z in range(6)]
            top = [jnp.where(k < 15, read(z, jnp.minimum(k + 1, 15)), 0.0) for z in range(6)]
            even, odd = [], []
            for j in range(3):
                even.append(jnp.where(lane < 64, now[j], pltpu.roll(now[j + 3], 64, 1)))
                odd.append(jnp.where(lane < 64, pltpu.roll(now[j], 64, 1), now[j + 3]))
            h_even = jnp.zeros((n, 128), F32)
            h_odd = jnp.zeros((n, 128), F32)
            for z in range(6):
                here = pltpu.roll(now[z], 65 + 2 * z, 1)
                h_even = jnp.where(lane == 2 * z, pltpu.roll(low[z], 1 + 2 * z, 1), h_even)
                h_even = jnp.where(lane == 2 * z + 1, here, h_even)
                h_odd = jnp.where(lane == 2 * z, here, h_odd)
                h_odd = jnp.where(lane == 2 * z + 1, pltpu.roll(top[z], 1 + 2 * z, 1), h_odd)
            return (even, h_even), (odd, h_odd)

        return pieces

    @pl.when(is_main)
    def _():
        get = cut(lambda z, k: Hf[pl.ds(z * 128 + k, 8, stride=16), :], 8)

        @pl.loop(0, 16)
        def _(k):
            for parity, (body, halo) in enumerate(get(k)):
                d = 2 * k + parity
                for j in range(3):
                    pk[d, j] = body[j]
                spread = pltpu.roll(halo, 0, 1, stride=16, stride_axis=0)
                hrow[d] = jnp.sum(spread, axis=0, keepdims=True)

    @pl.when(is_edge)
    def _():
        x_row = jnp.where(t == edges[0], 7, 0)
        get = cut(lambda z, k: Hf[pl.ds(z * 128 + x_row * 16 + k, 1), :], 1)

        @pl.loop(0, 16)
        def _(k):
            for parity, (body, halo) in enumerate(get(k)):
                d = 2 * k + parity
                for j in range(3):
                    ek[d, j] = body[j]
                ek[d, 3] = halo

    @pl.when(is_source)
    def _():
        pl.semaphore_wait(ready, n_tile - 1)

    def to_slab(d, i):
        own = jnp.int32(i) if isinstance(i, int) else i
        at = pl.multiple_of(own * 8 + 8, 8)
        return (
            pltpu.make_async_remote_copy(
                src_ref=pk.at[d],
                dst_ref=W.at[pl.ds(0, 3), pl.ds(at, 8)],
                send_sem=send_b.at[0],
                recv_sem=recv_b.at[0, own],
                device_id=(s, d),
                device_id_type=MESH,
            ),
            pltpu.make_async_remote_copy(
                src_ref=hrow.at[d],
                dst_ref=Ph.at[own],
                send_sem=send_b.at[1],
                recv_sem=recv_b.at[1, own],
                device_id=(s, d),
                device_id_type=MESH,
            ),
        )

    def edge_to_slab(d, i):
        own = jnp.int32(i) if isinstance(i, int) else i
        return pltpu.make_async_remote_copy(
            src_ref=ek.at[d],
            dst_ref=Pe.at[own],
            send_sem=send_b.at[0],
            recv_sem=recv_b.at[2, own],
            device_id=(s, d),
            device_id_type=MESH,
        )

    @pl.when(is_main)
    def _():
        own = t - main[0]

        @pl.loop(0, n_tile)
        def _(d):
            @pl.when(d != t)
            def _():
                for copy in to_slab(d, own):
                    copy.start()

        at = pl.multiple_of(own * 8 + 8, 8)
        W[0:3, pl.ds(at, 8), :] = pk[t]
        Ph[own] = hrow[t]

    @pl.when(is_edge)
    def _():
        own = jnp.where(t == edges[0], 0, 1)

        @pl.loop(0, n_tile)
        def _(d):
            @pl.when(d != t)
            def _():
                edge_to_slab(d, own).start()

        Pe[own] = ek[t]

    for z in range(4):
        for k in range(16):
            x_v[z, :, 128 * k : 128 * k + 128] = Hf[pl.ds((z + 1) * 128 + k, 8, stride=16), :]
    heat_copy = pltpu.make_async_copy(x_v, heat_out, out_sem.at[0])
    heat_copy.start()

    for a, b, copy in fine:

        @pl.when(there(-a, -b))
        def _():
            copy.wait_recv()

    for a, b, copy in fine:

        @pl.when(there(a, b))
        def _():
            copy.wait_send()

    r16 = lax.broadcasted_iota(jnp.int32, (16, 128), 0)
    l16 = lanes(16)
    both = col_in[...].reshape(16, 512)
    tn = (((0,), (0,)), ((), ()))
    s_rad = jnp.where(((r16 == 0) & (l16 == 0)) | ((r16 == 10) & (l16 == 127)), 1.0, 0.0)
    s_spd = jnp.where(((r16 == 1) & (l16 == 0)) | ((r16 == 11) & (l16 == 127)), 1.0, 0.0)
    side_rad[...] = lax.dot_general(
        both, s_rad, tn, precision=hi, preferred_element_type=F32
    ).reshape(8, 64, 128)
    side_spd[...] = lax.dot_general(
        both, s_spd, tn, precision=hi, preferred_element_type=F32
    ).reshape(8, 64, 128)
    for z in range(10):
        Gf[z, 0:8] = jnp.zeros((8, 128), F32)
        Gf[z, 72:80] = jnp.zeros((8, 128), F32)

    for i, q in enumerate(main):

        @pl.when(t != q)
        def _():
            for copy in to_slab(t, i):
                copy.wait_recv()

    for i, q in enumerate(edges):

        @pl.when(t != q)
        def _():
            edge_to_slab(t, i).wait_recv()

    spot_of = (lane8 + 16 * pick_r) & 127
    for i in range(4):
        W[3, 8 + 8 * i : 16 + 8 * i] = lane_pick(jnp.broadcast_to(Ph[i], (8, 128)), spot_of)
    for j in range(4):
        W[j, 7:8] = Pe[0, j]
        W[j, 40:41] = Pe[1, j]

    Xf = X.reshape(4 * 64, 128)
    for j in range(4):
        low, mid, top = W[j, 7:39], 0.75 * W[j, 8:40], W[j, 9:41]
        Xf[pl.ds(64 * j, 32, stride=2), :] = 0.25 * low + mid
        Xf[pl.ds(64 * j + 1, 32, stride=2), :] = mid + 0.25 * top

    lane = lanes(64)
    half = lane >> 1
    near = jnp.clip(half + jnp.where((lane & 1) == 1, 1, -1), 0, 63)
    rim = (lane == 0) | (lane == 127)
    fine_y, side_y = [], []
    for z in range(6):
        base = 0 if z < 3 else 64
        x = X[z % 3]
        u = lane_pick(x, half + base)
        h = lane_pick(X[3], jnp.where(lane == 127, 2 * z + 1, 2 * z))
        v = jnp.where(rim, h, lane_pick(x, near + base))
        fine_y.append(0.75 * u + 0.25 * v)
        side_y.append(0.75 * h + 0.25 * u)

    def at_height(f, zf):
        z = zf // 2
        if zf % 2 == 0:
            return 0.25 * f[z] + 0.75 * f[z + 1]
        return 0.75 * f[z + 1] + 0.25 * f[z + 2]

    def grow(temp, speed, radius):
        under = jnp.maximum(1.0 - temp, 0.0)
        return radius + speed * under * under

    for zf in range(-1, 9):
        if zf == -1:
            sp, ra = face_spd[0], face_rad[0]
        elif zf == 8:
            sp, ra = face_spd[1], face_rad[1]
        else:
            sp, ra = spd[zf], rad[zf]
        Gf[zf + 1, 8:72] = grow(at_height(fine_y, zf), sp, ra)
    for zf in range(8):
        side = grow(at_height(side_y, zf), side_spd[zf], side_rad[zf])
        c = Gf[zf + 1, 8:72]
        near_y = jnp.maximum(
            jnp.where(lane == 0, side, pltpu.roll(c, 1, 1)),
            jnp.where(lane == 127, side, pltpu.roll(c, 127, 1)),
        )
        near_x = jnp.maximum(Gf[zf + 1, 7:71], Gf[zf + 1, 9:73])
        near_z = jnp.maximum(Gf[zf, 8:72], Gf[zf + 2, 8:72])
        env[zf] = jnp.maximum(c, jnp.maximum(jnp.maximum(near_x, near_y), near_z) - 0.5)
    env_copy = pltpu.make_async_copy(env, grown_out, out_sem.at[1])
    env_copy.start()

    @pl.when(is_main)
    def _():
        @pl.loop(0, n_tile - 1)
        def _(d):
            for copy in to_slab(d, 0):
                copy.wait_send()

    @pl.when(is_edge)
    def _():
        @pl.loop(0, n_tile - 1)
        def _(d):
            edge_to_slab(d, 0).wait_send()

    heat_copy.wait()
    env_copy.wait()


def local(temperature, spot, labels, radius, position, seeds):
    n_slab, n_tile = lax.axis_size("slab"), lax.axis_size("tile")
    any_spec = pl.BlockSpec(memory_space=pl.ANY)
    vm = pltpu.VMEM
    dma = pltpu.SemaphoreType.DMA
    body = lambda *refs: kernel(n_slab, n_tile, *refs)
    return pl.pallas_call(
        body,
        out_shape=(
            jax.ShapeDtypeStruct((4, 8, 2048), F32),
            jax.ShapeDtypeStruct((8, 64, 128), F32),
        ),
        in_specs=[any_spec] * 6,
        out_specs=(any_spec, any_spec),
        scratch_shapes=[
            vm((4, 8, 2048), F32),
            pltpu.SMEM((2, 2), jnp.int32),
            vm((8, 64, 128), jnp.int32),
            vm((8, 64, 128), F32),
            vm((64,), jnp.int32),
            vm((64,), jnp.int32),
            vm((8, 64, 128), F32),
            vm((10, 12, 16, 128), F32),
            vm((10, 12, 16, 128), F32),
            vm((8, 10, 16, 128), F32),
            vm((6, 8, 16, 128), F32),
            vm((2, 12, 16, 128), F32),
            vm((8, 16, 128), F32),
            vm((32, 3, 8, 128), F32),
            vm((32, 1, 128), F32),
            vm((32, 4, 1, 128), F32),
            vm((4, 48, 128), F32),
            vm((4, 1, 128), F32),
            vm((2, 4, 1, 128), F32),
            vm((4, 64, 128), F32),
            vm((2, 64, 128), F32),
            vm((2, 64, 128), F32),
            vm((8, 512), F32),
            vm((2, 8, 512), F32),
            vm((8, 64, 128), F32),
            vm((8, 64, 128), F32),
            vm((10, 80, 128), F32),
            vm((8, 64, 128), F32),
            dma((6,)),
            dma((2,)),
            dma((14,)),
            dma((14,)),
            dma((2,)),
            dma((3, 4)),
            pltpu.SemaphoreType.REGULAR,
        ],
        compiler_params=pltpu.CompilerParams(collective_id=0, has_side_effects=True),
        name="build_step",
    )(temperature, spot, labels, radius, position, seeds)


def solution(mesh):
    return jax.shard_map(
        local,
        mesh=mesh,
        in_specs=(
            P("slab", "tile", None),
            P(),
            P("slab", None, "tile"),
            P("slab", None, "tile"),
            P(("slab", "tile")),
            P(("slab", "tile")),
        ),
        out_specs=(P("slab", "tile", None), P("slab", None, "tile")),
        check_vma=False,
    )
```

time: 108 us -> 36.6 us (0.34)
  the two profiles are of different devices: /device:TPU:26 before, /device:TPU:31 now
where the time goes in v1:
time: 36.6 us; the launch traced here: 36.4 us
  Pallas kernels  33.3 us (91%)
  local copies, waits for them, and re-layouts  2.42 us (7%)
  between operations  0.65 us (2%)
    pallas_call x1, Pallas kernels, local(): pl.pallas_call(body, out_shape=(jax.ShapeDtypeStruct((4, 8, 2048), F32),...  33.3 us
    unnamed x4, local copies, waits for them, and re-layouts  2.42 us

profile of v1, /device:TPU:31, one launch (start us, length us, event | category | flops | bytes accessed | tf_op | source)
XLA Modules:
  0.0 36.4 jit_solution(5486492739289365382)
XLA Ops:
  0.6 33.3 %build_step.1 = (f32[4,8,2048]{2,1,0:T(8,128)}, f32[8,64,128]{2,1,0:T(8,128)}) custom-call(f32[4,8,2048]{2,1,0:T(8,128)} %refs_0_.1, s32[2,2]{1,0:T(2,128)} %refs_1_.1, s32[8,64,128]{2,1,0:T(8,128)} %refs_2_.1, f32[8,64,128]{2,1,0:T(8,128)} %refs_3_.1, s32[64]{0:T(128)} %refs_4_.1, s32[64]{0:T(128)} %refs_5_.1), custom_call_target="tpu_custom_call" | custom-call | tf_op jit(solution)/shard_map/build_step/pallas_call | solution.py:608
  34.0 0.0 copy-start
  34.0 1.7 %copy.10 = f32[4,8,2048]{2,1,0:T(8,128)} copy(f32[4,8,2048]{2,1,0:T(8,128)} %get-tuple-element.4) | data formatting | bytes 524288
  35.7 0.0 copy-done
  35.7 0.7 %copy.11 = f32[8,64,128]{2,1,0:T(8,128)} copy(f32[8,64,128]{2,1,0:T(8,128)S(1)} %copy-done) | data formatting | bytes 524288
Async XLA Ops:
  34.0 1.7 %copy-start = (f32[8,64,128]{2,1,0:T(8,128)S(1)}, f32[8,64,128]{2,1,0:T(8,128)}, u32[]{:S(2)}) copy-start(f32[8,64,128]{2,1,0:T(8,128)} %get-tuple-element.5) | copy-start | bytes 786436

commit v2 on v1

v2 whole, which is shorter than its diff:
```python
import jax
import jax.numpy as jnp
from jax import lax
from jax.experimental import pallas as pl
from jax.experimental.pallas import tpu as pltpu
from jax.sharding import PartitionSpec as P

HEAT_RATE = 0.1
SOURCE_POWER = 1.5
BEAM_RADIUS_SQ = 36.0
DEPTH_SCALE = 3.0
GOLDEN_ANGLE = 2.39996323
MESH = pl.DeviceIdType.MESH
NZ = 8
F32 = jnp.float32
NEIGHBOURS = [(a, b) for a in (-1, 0, 1) for b in (-1, 0, 1) if (a, b) != (0, 0)]


def lanes(rows):
    return lax.broadcasted_iota(jnp.int32, (rows, 128), 1)


def lane_pick(x, index):
    return jnp.take_along_axis(x, index, axis=1)


def conductance(v):
    return 0.5 * HEAT_RATE * 1.5 - (0.25 * HEAT_RATE) / (1.0 + v * v)


def next_along_y(x, last):
    r = pltpu.roll(x, 127, 2)
    up = pltpu.roll(r, 15, 1)
    lane = lax.broadcasted_iota(jnp.int32, x.shape, 2)
    row = lax.broadcasted_iota(jnp.int32, x.shape, 1)
    up = jnp.where(row == 15, last, up)
    return jnp.where(lane == 127, up, r)


def before_along_y(x, first):
    r = pltpu.roll(x, 1, 2)
    down = pltpu.roll(r, 1, 1)
    lane = lax.broadcasted_iota(jnp.int32, x.shape, 2)
    row = lax.broadcasted_iota(jnp.int32, x.shape, 1)
    down = jnp.where(row == 0, first, down)
    return jnp.where(lane == 0, down, r)


def heat_step(src, cond, dst, plane, depth, count_z, count_x, offset_x):
    def conductances(z, c):
        cond[z] = conductance(src[z])
        return c

    lax.fori_loop(0, count_z, conductances, 0)

    def layer(z, c):
        v = src[z + 1]
        p = cond[z + 1]
        flux_x = (p[:-1] + p[1:]) * (v[1:] - v[:-1])
        inner = slice(1, count_x - 1)
        vc, pc = v[inner], p[inner]
        total = flux_x[1:] - flux_x[:-1]
        total += (pc + cond[z, 1 : count_x - 1]) * (src[z, 1 : count_x - 1] - vc)
        total += (pc + cond[z + 2, 1 : count_x - 1]) * (src[z + 2, 1 : count_x - 1] - vc)
        outside = 0.5 * HEAT_RATE
        flux_y = (pc + next_along_y(pc, outside)) * (next_along_y(vc, 0.0) - vc)
        edge = (pc + outside) * vc
        low = jnp.broadcast_to(edge[:, 0:1, 0:1], vc.shape)
        total += flux_y - before_along_y(flux_y, low)
        source = plane[offset_x : offset_x + count_x - 2] * depth[z]
        dst[z] = vc + total + source
        return c

    lax.fori_loop(0, count_z - 2, layer, 0)


def window_step(src, cond, dst, plane, depth, count_z, keep):
    for z in range(count_z):
        cond[z] = conductance(src[z])
    for z in range(count_z - 2):
        v, p = src[z + 1, 8:56], cond[z + 1, 8:56]
        total = (p + cond[z, 8:56]) * (src[z, 8:56] - v)
        total += (p + cond[z + 2, 8:56]) * (src[z + 2, 8:56] - v)
        total += (p + cond[z + 1, 7:55]) * (src[z + 1, 7:55] - v)
        total += (p + cond[z + 1, 9:57]) * (src[z + 1, 9:57] - v)
        total += (p + pltpu.roll(p, 1, 1)) * (pltpu.roll(v, 1, 1) - v)
        total += (p + pltpu.roll(p, 127, 1)) * (pltpu.roll(v, 127, 1) - v)
        at = jnp.broadcast_to(depth[z, 0:1, :], v.shape)
        dst[z, 8:56] = jnp.where(keep, v + total + plane * at, 0.0)


def kernel(
    n_slab,
    n_tile,
    x_in,
    spot_in,
    lab_in,
    rad_in,
    pos_in,
    seed_in,
    heat_out,
    grown_out,
    x_v,
    spot,
    lab,
    rad,
    pos,
    seed,
    spd,
    E,
    PE,
    M,
    H,
    plane,
    depth,
    pk_own,
    pk_out,
    in_own,
    in_out,
    in_sib,
    rl_own,
    rl_out,
    V,
    PV,
    VM,
    VH,
    X,
    face_rad,
    face_spd,
    cols,
    col_in,
    side_rad,
    side_spd,
    Gf,
    env,
    in_sem,
    out_sem,
    send_a,
    recv_a,
    send_b,
    recv_b,
    recv_r,
    send_r,
):
    s = lax.axis_index("slab")
    t = lax.axis_index("tile")
    first = n_tile // 2 - 3
    sources = tuple(range(first, first + 6))
    is_source = (t >= first) & (t < first + 6)
    n_col = n_tile // NZ
    col, pos_z = t // NZ, t % NZ
    odd = s % 2 == 1
    sib = jnp.where(odd, s - 1, s + 1)
    outer = jnp.where(odd, s + 1, s - 1)
    has_outer = (outer >= 0) & (outer < n_slab)

    def sender_of(q):
        return jnp.where((col - q // NZ) % 2 == 0, q, col * NZ + q % NZ)

    relayed = jnp.int32(0)
    is_relay = jnp.bool_(False)
    for i, q in enumerate(sources):
        mine = (pos_z == q % NZ) & ((col - q // NZ) % 2 != 0)
        relayed = jnp.where(mine, i, relayed)
        is_relay = is_relay | mine

    def there(a, b):
        c = jnp.bool_(True)
        if a == -1:
            c = c & (s > 0)
        if a == 1:
            c = c & (s < n_slab - 1)
        if b == -1:
            c = c & (t > 0)
        if b == 1:
            c = c & (t < n_tile - 1)
        return c

    loads = [
        pltpu.make_async_copy(a, b, in_sem.at[i])
        for i, (a, b) in enumerate(
            (
                (x_in, x_v),
                (lab_in, lab),
                (rad_in, rad),
                (spot_in, spot),
                (pos_in, pos),
                (seed_in, seed),
            )
        )
    ]
    for c in loads:
        c.start()

    bar = pltpu.get_barrier_semaphore()
    count = jnp.int32(0)
    for a, b in NEIGHBOURS:
        c = there(a, b)

        @pl.when(c)
        def _():
            pl.semaphore_signal(bar, inc=1, device_id=(s + a, t + b), device_id_type=MESH)

        count = count + c.astype(jnp.int32)
    for q in sources:
        sender = sender_of(q)

        @pl.when(sender != t)
        def _():
            pl.semaphore_signal(bar, inc=1, device_id=(s, sender), device_id_type=MESH)

        @pl.when(has_outer)
        def _():
            pl.semaphore_signal(bar, inc=1, device_id=(outer, sender), device_id_type=MESH)

    @pl.when(is_relay)
    def _():
        pl.semaphore_signal(bar, inc=1, device_id=(s, first + relayed), device_id_type=MESH)

    half_tiles = n_tile // 2
    count = count + jnp.where(
        is_source, half_tiles - 1 + n_col // 2 + jnp.where(has_outer, half_tiles, 0), 0
    )
    count = count + jnp.where(is_relay, NZ - 1 + jnp.where(has_outer, NZ, 0), 0)

    @pl.when(s == 0)
    def _():
        E[0:2] = jnp.zeros((2,) + E.shape[1:], F32)
        V[0:3] = jnp.zeros((3,) + V.shape[1:], F32)
        face_rad[0] = jnp.zeros((64, 128), F32)
        face_spd[0] = jnp.zeros((64, 128), F32)

    @pl.when(s == n_slab - 1)
    def _():
        E[6:8] = jnp.zeros((2,) + E.shape[1:], F32)
        V[7:10] = jnp.zeros((3,) + V.shape[1:], F32)
        face_rad[1] = jnp.zeros((64, 128), F32)
        face_spd[1] = jnp.zeros((64, 128), F32)

    @pl.when(t == 0)
    def _():
        E[:, 0:2] = jnp.zeros((8, 2) + E.shape[2:], F32)
        col_in[0] = jnp.zeros(col_in.shape[1:], F32)

    @pl.when(t == n_tile - 1)
    def _():
        E[:, 10:12] = jnp.zeros((8, 2) + E.shape[2:], F32)
        col_in[1] = jnp.zeros(col_in.shape[1:], F32)

    loads[0].wait()
    flat = E.reshape(8 * 12 * 16, 128)
    for z in range(4):
        for k in range(16):
            row = ((z + 2) * 12 + 2) * 16 + k
            flat[pl.ds(row, 8, stride=16), :] = x_v[z, :, 128 * k : 128 * k + 128]

    lane8 = lanes(8)
    left = lane8 < 64

    @pl.when(is_source)
    def _():
        def read(z, k):
            if k < 0 or k > 15:
                return jnp.zeros((8, 128), F32)
            return x_v[z, :, 128 * k : 128 * k + 128]

        for k in range(16):
            now = [read(z, k) for z in range(4)]
            turned = [pltpu.roll(v, 64, 1) for v in now]
            h_even = jnp.zeros((8, 128), F32)
            h_odd = jnp.zeros((8, 128), F32)
            for z in range(4):
                low, top = read(z, k - 1), read(z, k + 1)
                here = pltpu.roll(now[z], 67 + 6 * z, 1)
                low = pltpu.roll(low, 3 + 6 * z, 1)
                top = pltpu.roll(top, 3 + 6 * z, 1)
                one = (lane8 >= 6 * z) & (lane8 < 6 * z + 3)
                two = (lane8 >= 6 * z + 3) & (lane8 < 6 * z + 6)
                h_even = jnp.where(one, low, jnp.where(two, here, h_even))
                h_odd = jnp.where(one, here, jnp.where(two, top, h_odd))
            for parity, lo, up, halo in ((0, now, turned, h_even), (1, turned, now, h_odd)):
                d = 2 * k + parity
                far = pltpu.roll(halo, 64, 1)
                pk_own[d, 0] = jnp.where(left, lo[0], up[2])
                pk_own[d, 1] = jnp.where(left, lo[1], up[3])
                pk_own[d, 2] = halo
                pk_out[d, 0] = jnp.where(
                    left, jnp.where(odd, lo[1], lo[0]), jnp.where(odd, up[2], up[1])
                )
                pk_out[d, 1] = jnp.where(left, jnp.where(odd, lo[3], lo[2]), far)

    pl.semaphore_wait(bar, count)

    halos = []
    for a, b in NEIGHBOURS:
        zs = {0: (2, 4, 2), -1: (2, 2, 6), 1: (4, 2, 0)}[a]
        xs = {0: (2, 8, 2), -1: (2, 2, 10), 1: (8, 2, 0)}[b]
        if a != 0 and b != 0:
            zs = {-1: (2, 1, 6), 1: (5, 1, 1)}[a]
            xs = {-1: (2, 1, 10), 1: (9, 1, 1)}[b]
        k = len(halos)
        halos.append(
            (
                a,
                b,
                pltpu.make_async_remote_copy(
                    src_ref=E.at[pl.ds(zs[0], zs[1]), pl.ds(xs[0], xs[1])],
                    dst_ref=E.at[pl.ds(zs[2], zs[1]), pl.ds(xs[2], xs[1])],
                    send_sem=send_a.at[k],
                    recv_sem=recv_a.at[k],
                    device_id=(s + a, t + b),
                    device_id_type=MESH,
                ),
            )
        )
    for a, b, copy in sorted(halos, key=lambda h: -h[1]):

        @pl.when(there(a, b))
        def _():
            copy.start()

    def send(kind, src, d, i):
        own = jnp.int32(i) if isinstance(i, int) else i
        return pltpu.make_async_remote_copy(
            src_ref=src,
            dst_ref=(in_own, in_out)[kind].at[own],
            send_sem=send_b.at[kind],
            recv_sem=recv_b.at[kind, own],
            device_id=((s, outer)[kind], d),
            device_id_type=MESH,
        )

    def to_relay(kind, d, at, z):
        return pltpu.make_async_remote_copy(
            src_ref=(pk_own, pk_out)[kind].at[d],
            dst_ref=(rl_own, rl_out)[kind].at[z],
            send_sem=send_b.at[kind],
            recv_sem=recv_r.at[kind, z],
            device_id=(s, at),
            device_id_type=MESH,
        )

    def to_sibling(i):
        return pltpu.make_async_remote_copy(
            src_ref=in_own.at[i],
            dst_ref=in_sib.at[i],
            send_sem=send_r.at[0],
            recv_sem=recv_b.at[2, i],
            device_id=(sib, t),
            device_id_type=MESH,
        )

    @pl.when(is_source)
    def _():
        own = t - first

        @pl.loop(0, NZ)
        def _(z):
            for c in range(0, n_col, 2):
                d = (col + c + 1) % n_col * NZ + z
                at = (col + c + 1) % n_col * NZ + pos_z
                to_relay(0, d, at, z).start()

                @pl.when(has_outer)
                def _():
                    to_relay(1, d, at, z).start()

            for c in range(0, n_col, 2):
                d = (col + c) % n_col * NZ + z

                @pl.when(d != t)
                def _():
                    send(0, pk_own.at[d], d, own).start()

                @pl.when(has_outer)
                def _():
                    send(1, pk_out.at[d], d, own).start()

        in_own[own] = pk_own[t]

    for c in loads[1:]:
        c.wait()
    place = pos[...].reshape(1, 64)
    value = ((seed[...].reshape(1, 64) & 63) + 1).astype(F32)
    rows = lax.broadcasted_iota(jnp.int32, (512, 64), 0)
    cells = lax.broadcasted_iota(jnp.int32, (128, 64), 0)
    in_row = jnp.where(rows == (place >> 7), 1.0, 0.0).astype(jnp.bfloat16)
    in_lane = jnp.where(cells == (place & 127), value, 0.0).astype(jnp.bfloat16)
    named = lax.dot_general(
        in_row, in_lane, (((1,), (1,)), ((), ())), preferred_element_type=F32
    ).reshape(8, 64, 128)
    theta = GOLDEN_ANGLE * lanes(8).astype(F32)
    table = 1.0 + 0.5 * jnp.cos(4.0 * theta)
    table = jnp.broadcast_to(table[0:1], (64, 128))
    for z in range(8):
        grain = jnp.where(named[z] > 0.5, named[z].astype(jnp.int32) - 1, lab[z] & 63)
        spd[z] = lane_pick(table, grain)

    pick_r = lax.broadcasted_iota(jnp.int32, (8, 128), 0)
    nt = (((1,), (1,)), ((), ()))
    e_rad = jnp.where(
        ((pick_r == 0) & (lane8 == 127)) | ((pick_r == 2) & (lane8 == 0)), 1.0, 0.0
    )
    e_spd = jnp.where(
        ((pick_r == 1) & (lane8 == 127)) | ((pick_r == 3) & (lane8 == 0)), 1.0, 0.0
    )
    hi = lax.Precision.HIGHEST
    cols[...] = lax.dot_general(
        e_rad, rad[...].reshape(512, 128), nt, precision=hi, preferred_element_type=F32
    ) + lax.dot_general(
        e_spd, spd[...].reshape(512, 128), nt, precision=hi, preferred_element_type=F32
    )

    sides = []
    lane48 = lanes(48)
    wy = t * 64 + lane48 - jnp.where(lane48 < 100, 0, 128)
    wx = lax.broadcasted_iota(jnp.int32, (48, 128), 0) + first * 8
    for step in range(2):
        row = lax.broadcasted_iota(jnp.int32, (12, 16, 128), 0)
        y = lax.broadcasted_iota(jnp.int32, (12, 16, 128), 1) * 128
        y = y + lax.broadcasted_iota(jnp.int32, (12, 16, 128), 2)
        xd = (t * 8 - 2 + row - spot[step, 0]).astype(F32)
        yd = (y - spot[step, 1]).astype(F32)
        plane[step] = SOURCE_POWER * jnp.exp(-(xd * xd + yd * yd) / BEAM_RADIUS_SQ)
        xd = (wx - spot[step, 0]).astype(F32)
        yd = (wy - spot[step, 1]).astype(F32)
        sides.append(SOURCE_POWER * jnp.exp(-(xd * xd + yd * yd) / BEAM_RADIUS_SQ))
    level = lax.broadcasted_iota(jnp.int32, (8, 16, 128), 0) + (s * 4 - 2)
    depth[...] = jnp.exp(-(n_slab * 4 - 1 - level).astype(F32) / DEPTH_SCALE)

    fine = []
    k0 = len(NEIGHBOURS)
    for a, z in ((1, 7), (-1, 0)):
        slot = 0 if a == 1 else 1
        fine.append((a, 0, rad.at[z], face_rad.at[slot], (s + a, t)))
        fine.append((a, 0, spd.at[z], face_spd.at[slot], (s + a, t)))
    for b in (1, -1):
        slot = 0 if b == 1 else 1
        fine.append((0, b, cols, col_in.at[slot], (s, t + b)))
    fine = [
        (
            a,
            b,
            pltpu.make_async_remote_copy(
                src_ref=src,
                dst_ref=dst,
                send_sem=send_a.at[k0 + i],
                recv_sem=recv_a.at[k0 + i],
                device_id=to,
                device_id_type=MESH,
            ),
        )
        for i, (a, b, src, dst, to) in enumerate(fine)
    ]
    for a, b, copy in fine:

        @pl.when(there(a, b))
        def _():
            copy.start()

    @pl.when(is_relay)
    def _():
        @pl.loop(0, NZ)
        def _(z):
            d = col * NZ + z
            to_relay(0, d, t, z).wait_recv()

            @pl.when(d != t)
            def _():
                send(0, rl_own.at[z], d, relayed).start()

            @pl.when(d == t)
            def _():
                in_own[relayed] = rl_own[z]

            @pl.when(has_outer)
            def _():
                to_relay(1, d, t, z).wait_recv()
                send(1, rl_out.at[z], d, relayed).start()

    for a, b, copy in halos:

        @pl.when(there(-a, -b))
        def _():
            copy.wait_recv()

    for a, b, copy in halos:

        @pl.when(there(a, b))
        def _():
            copy.wait_send()

    heat_step(E, PE, M, plane.at[0], depth.at[1:7], 8, 12, 1)

    @pl.when(s == 0)
    def _():
        M[0:1] = jnp.zeros((1,) + M.shape[1:], F32)

    @pl.when(s == n_slab - 1)
    def _():
        M[5:6] = jnp.zeros((1,) + M.shape[1:], F32)

    @pl.when(t == 0)
    def _():
        M[:, 0:1] = jnp.zeros((6, 1) + M.shape[2:], F32)

    @pl.when(t == n_tile - 1)
    def _():
        M[:, 9:10] = jnp.zeros((6, 1) + M.shape[2:], F32)

    heat_step(M, PE.at[0:6, 0:10], H, plane.at[1], depth.at[2:6], 6, 10, 2)

    Hf = H.reshape(4 * 8 * 16, 128)
    for z in range(4):
        for k in range(16):
            x_v[z, :, 128 * k : 128 * k + 128] = Hf[pl.ds(z * 128 + k, 8, stride=16), :]
    heat_copy = pltpu.make_async_copy(x_v, heat_out, out_sem.at[0])
    heat_copy.start()

    for a, b, copy in fine:

        @pl.when(there(-a, -b))
        def _():
            copy.wait_recv()

    for a, b, copy in fine:

        @pl.when(there(a, b))
        def _():
            copy.wait_send()

    r16 = lax.broadcasted_iota(jnp.int32, (16, 128), 0)
    l16 = lanes(16)
    both = col_in[...].reshape(16, 512)
    tn = (((0,), (0,)), ((), ()))
    s_rad = jnp.where(((r16 == 0) & (l16 == 0)) | ((r16 == 10) & (l16 == 127)), 1.0, 0.0)
    s_spd = jnp.where(((r16 == 1) & (l16 == 0)) | ((r16 == 11) & (l16 == 127)), 1.0, 0.0)
    side_rad[...] = lax.dot_general(
        both, s_rad, tn, precision=hi, preferred_element_type=F32
    ).reshape(8, 64, 128)
    side_spd[...] = lax.dot_general(
        both, s_spd, tn, precision=hi, preferred_element_type=F32
    ).reshape(8, 64, 128)
    for z in range(10):
        Gf[z, 0:8] = jnp.zeros((8, 128), F32)
        Gf[z, 72:80] = jnp.zeros((8, 128), F32)

    for i, q in enumerate(sources):

        @pl.when(sender_of(q) != t)
        def _():
            send(0, pk_own.at[0], t, i).wait_recv()

        to_sibling(i).start()

        @pl.when(has_outer)
        def _():
            send(1, pk_out.at[0], t, i).wait_recv()

    far_lane = jnp.where(lane8 >= 100, lane8 - 125, lane8 - 61)

    def put(i, z, tile, high, halo, base):
        body = pltpu.roll(tile, 64, 1) if high else tile
        around = lane_pick(halo, (far_lane + base) & 127)
        V[z, 8 + 8 * i : 16 + 8 * i] = jnp.where(left, body, around)

    for i in range(6):
        for z in range(4):
            put(i, 3 + z, in_own[i, z % 2], z >= 2, in_own[i, 2], 6 * z)

    @pl.when(has_outer)
    def _():
        at = jnp.where(odd, 7, 0)
        base = 64 + jnp.where(odd, 0, 6)
        for i in range(6):
            for z in range(3):
                put(i, at + z, in_out[i, z // 2], z == 1, in_out[i, 1], base + 6 * z)

    for i in range(6):
        to_sibling(i).wait_recv()

    @pl.when(odd)
    def _():
        for i in range(6):
            for z in range(3):
                put(i, z, in_sib[i, (z + 1) % 2], z >= 1, in_sib[i, 2], 6 * (z + 1))

    @pl.when(jnp.logical_not(odd))
    def _():
        for i in range(6):
            for z in range(3):
                put(i, 7 + z, in_sib[i, z % 2], z >= 2, in_sib[i, 2], 6 * z)

    keep = (lane48 < 64) | ((lane48 < 100) & (t < n_tile - 1)) | ((lane48 >= 100) & (t > 0))
    window_step(V, PV, VM, sides[0], depth, 10, keep)

    @pl.when(s == 0)
    def _():
        VM[0:2] = jnp.zeros((2,) + VM.shape[1:], F32)

    @pl.when(s == n_slab - 1)
    def _():
        VM[6:8] = jnp.zeros((2,) + VM.shape[1:], F32)

    window_step(VM, PV.at[0:8], VH, sides[1], depth.at[1:7], 8, keep)

    @pl.when(s == 0)
    def _():
        VH[0] = jnp.zeros(VH.shape[1:], F32)

    @pl.when(s == n_slab - 1)
    def _():
        VH[5] = jnp.zeros(VH.shape[1:], F32)

    Xf = X.reshape(6 * 64, 128)
    for z in range(6):
        low, mid, top = VH[z, 15:47], 0.75 * VH[z, 16:48], VH[z, 17:49]
        Xf[pl.ds(64 * z, 32, stride=2), :] = 0.25 * low + mid
        Xf[pl.ds(64 * z + 1, 32, stride=2), :] = mid + 0.25 * top

    lane = lanes(64)
    half = lane >> 1
    near = (half + jnp.where((lane & 1) == 1, 1, -1)) & 127
    fine_y, side_y = [], []
    for z in range(6):
        u = lane_pick(X[z], half)
        v = lane_pick(X[z], near)
        fine_y.append(0.75 * u + 0.25 * v)
        side_y.append(0.75 * v + 0.25 * u)

    def at_height(f, zf):
        z = zf // 2
        if zf % 2 == 0:
            return 0.25 * f[z] + 0.75 * f[z + 1]
        return 0.75 * f[z + 1] + 0.25 * f[z + 2]

    def grow(temp, speed, radius):
        under = jnp.maximum(1.0 - temp, 0.0)
        return radius + speed * under * under

    for zf in range(-1, 9):
        if zf == -1:
            sp, ra = face_spd[0], face_rad[0]
        elif zf == 8:
            sp, ra = face_spd[1], face_rad[1]
        else:
            sp, ra = spd[zf], rad[zf]
        Gf[zf + 1, 8:72] = grow(at_height(fine_y, zf), sp, ra)
    for zf in range(8):
        side = grow(at_height(side_y, zf), side_spd[zf], side_rad[zf])
        c = Gf[zf + 1, 8:72]
        near_y = jnp.maximum(
            jnp.where(lane == 0, side, pltpu.roll(c, 1, 1)),
            jnp.where(lane == 127, side, pltpu.roll(c, 127, 1)),
        )
        near_x = jnp.maximum(Gf[zf + 1, 7:71], Gf[zf + 1, 9:73])
        near_z = jnp.maximum(Gf[zf, 8:72], Gf[zf + 2, 8:72])
        env[zf] = jnp.maximum(c, jnp.maximum(jnp.maximum(near_x, near_y), near_z) - 0.5)
    env_copy = pltpu.make_async_copy(env, grown_out, out_sem.at[1])
    env_copy.start()

    for i in range(6):
        to_sibling(i).wait_send()

    n_own = jnp.where(is_source, n_tile - 1, 0) + jnp.where(is_relay, NZ - 1, 0)
    n_out = jnp.where(is_source, n_tile, 0) + jnp.where(is_relay, NZ, 0)

    @pl.loop(0, n_own)
    def _(d):
        send(0, pk_own.at[0], t, 0).wait_send()

    @pl.when(has_outer)
    def _():
        @pl.loop(0, n_out)
        def _(d):
            send(1, pk_out.at[0], t, 0).wait_send()

    heat_copy.wait()
    env_copy.wait()


def local(temperature, spot, labels, radius, position, seeds):
    n_slab, n_tile = lax.axis_size("slab"), lax.axis_size("tile")
    any_spec = pl.BlockSpec(memory_space=pl.ANY)
    vm = pltpu.VMEM
    dma = pltpu.SemaphoreType.DMA
    body = lambda *refs: kernel(n_slab, n_tile, *refs)
    return pl.pallas_call(
        body,
        out_shape=(
            jax.ShapeDtypeStruct((4, 8, 2048), F32),
            jax.ShapeDtypeStruct((8, 64, 128), F32),
        ),
        in_specs=[any_spec] * 6,
        out_specs=(any_spec, any_spec),
        scratch_shapes=[
            vm((4, 8, 2048), F32),
            pltpu.SMEM((2, 2), jnp.int32),
            vm((8, 64, 128), jnp.int32),
            vm((8, 64, 128), F32),
            vm((64,), jnp.int32),
            vm((64,), jnp.int32),
            vm((8, 64, 128), F32),
            vm((8, 12, 16, 128), F32),
            vm((8, 12, 16, 128), F32),
            vm((6, 10, 16, 128), F32),
            vm((4, 8, 16, 128), F32),
            vm((2, 12, 16, 128), F32),
            vm((8, 16, 128), F32),
            vm((32, 3, 8, 128), F32),
            vm((32, 2, 8, 128), F32),
            vm((6, 3, 8, 128), F32),
            vm((6, 2, 8, 128), F32),
            vm((6, 3, 8, 128), F32),
            vm((NZ, 3, 8, 128), F32),
            vm((NZ, 2, 8, 128), F32),
            vm((10, 64, 128), F32),
            vm((10, 64, 128), F32),
            vm((8, 64, 128), F32),
            vm((6, 64, 128), F32),
            vm((6, 64, 128), F32),
            vm((2, 64, 128), F32),
            vm((2, 64, 128), F32),
            vm((8, 512), F32),
            vm((2, 8, 512), F32),
            vm((8, 64, 128), F32),
            vm((8, 64, 128), F32),
            vm((10, 80, 128), F32),
            vm((8, 64, 128), F32),
            dma((6,)),
            dma((2,)),
            dma((14,)),
            dma((14,)),
            dma((2,)),
            dma((3, 6)),
            dma((2, NZ)),
            dma((1,)),
        ],
        compiler_params=pltpu.CompilerParams(collective_id=0, has_side_effects=True),
        name="build_step",
    )(temperature, spot, labels, radius, position, seeds)


def solution(mesh):
    return jax.shard_map(
        local,
        mesh=mesh,
        in_specs=(
            P("slab", "tile", None),
            P(),
            P("slab", None, "tile"),
            P("slab", None, "tile"),
            P(("slab", "tile")),
            P(("slab", "tile")),
        ),
        out_specs=(P("slab", "tile", None), P("slab", None, "tile")),
        check_vma=False,
    )
```

time: 36.6 us -> 29.6 us (0.81)
  the two profiles are of different devices: /device:TPU:31 before, /device:TPU:94 now
where the time goes in v2:
time: 29.6 us; the launch traced here: 29.4 us
  Pallas kernels  26.4 us (89%)
  local copies, waits for them, and re-layouts  2.42 us (8%)
  between operations  0.65 us (2%)
    pallas_call x1, Pallas kernels, local(): pl.pallas_call(body, out_shape=(jax.ShapeDtypeStruct((4, 8, 2048), F32),...  26.4 us
    unnamed x4, local copies, waits for them, and re-layouts  2.42 us

profile of v2, /device:TPU:94, one launch (start us, length us, event | category | flops | bytes accessed | tf_op | source)
XLA Modules:
  0.0 29.4 jit_solution(9622050453449997447)
XLA Ops:
  0.6 26.4 %build_step.1 = (f32[4,8,2048]{2,1,0:T(8,128)}, f32[8,64,128]{2,1,0:T(8,128)}) custom-call(f32[4,8,2048]{2,1,0:T(8,128)} %refs_0_.1, s32[2,2]{1,0:T(2,128)} %refs_1_.1, s32[8,64,128]{2,1,0:T(8,128)} %refs_2_.1, f32[8,64,128]{2,1,0:T(8,128)} %refs_3_.1, s32[64]{0:T(128)} %refs_4_.1, s32[64]{0:T(128)} %refs_5_.1), custom_call_target="tpu_custom_call" | custom-call | tf_op jit(solution)/shard_map/build_step/pallas_call | solution.py:688
  27.0 0.0 copy-start
  27.0 1.7 %copy.10 = f32[4,8,2048]{2,1,0:T(8,128)} copy(f32[4,8,2048]{2,1,0:T(8,128)} %get-tuple-element.4) | data formatting | bytes 524288
  28.7 0.0 copy-done
  28.7 0.7 %copy.11 = f32[8,64,128]{2,1,0:T(8,128)} copy(f32[8,64,128]{2,1,0:T(8,128)S(1)} %copy-done) | data formatting | bytes 524288
Async XLA Ops:
  27.0 1.7 %copy-start = (f32[8,64,128]{2,1,0:T(8,128)S(1)}, f32[8,64,128]{2,1,0:T(8,128)}, u32[]{:S(2)}) copy-start(f32[8,64,128]{2,1,0:T(8,128)} %get-tuple-element.5) | copy-start | bytes 786436

commit v3 on v2

--- a/solution.py
+++ b/solution.py
@@ -12,6 +12,7 @@
 GOLDEN_ANGLE = 2.39996323
 MESH = pl.DeviceIdType.MESH
 NZ = 8
+FIRST, EARLY = 2, 4
 F32 = jnp.float32
 NEIGHBOURS = [(a, b) for a in (-1, 0, 1) for b in (-1, 0, 1) if (a, b) != (0, 0)]
 
@@ -46,32 +47,33 @@
     return jnp.where(lane == 0, down, r)
 
 
-def heat_step(src, cond, dst, plane, depth, count_z, count_x, offset_x):
+def heat_step(src, cond, dst, plane, depth, count_z, first_x, last_x, offset_x, fill, unroll):
+    wide, inner = slice(first_x, last_x + 2), slice(first_x + 1, last_x + 1)
+
     def conductances(z, c):
-        cond[z] = conductance(src[z])
+        cond[z, fill] = conductance(src[z, fill])
         return c
 
-    lax.fori_loop(0, count_z, conductances, 0)
+    lax.fori_loop(0, count_z, conductances, 0, unroll=unroll)
 
     def layer(z, c):
-        v = src[z + 1]
-        p = cond[z + 1]
+        v = src[z + 1, wide]
+        p = cond[z + 1, wide]
         flux_x = (p[:-1] + p[1:]) * (v[1:] - v[:-1])
-        inner = slice(1, count_x - 1)
-        vc, pc = v[inner], p[inner]
+        vc, pc = v[1:-1], p[1:-1]
         total = flux_x[1:] - flux_x[:-1]
-        total += (pc + cond[z, 1 : count_x - 1]) * (src[z, 1 : count_x - 1] - vc)
-        total += (pc + cond[z + 2, 1 : count_x - 1]) * (src[z + 2, 1 : count_x - 1] - vc)
+        total += (pc + cond[z, inner]) * (src[z, inner] - vc)
+        total += (pc + cond[z + 2, inner]) * (src[z + 2, inner] - vc)
         outside = 0.5 * HEAT_RATE
         flux_y = (pc + next_along_y(pc, outside)) * (next_along_y(vc, 0.0) - vc)
         edge = (pc + outside) * vc
         low = jnp.broadcast_to(edge[:, 0:1, 0:1], vc.shape)
         total += flux_y - before_along_y(flux_y, low)
-        source = plane[offset_x : offset_x + count_x - 2] * depth[z]
-        dst[z] = vc + total + source
+        source = plane[offset_x + first_x : offset_x + last_x] * depth[z]
+        dst[z, first_x:last_x] = vc + total + source
         return c
 
-    lax.fori_loop(0, count_z - 2, layer, 0)
+    lax.fori_loop(0, count_z - 2, layer, 0, unroll=unroll)
 
 
 def window_step(src, cond, dst, plane, depth, count_z, keep):
@@ -110,6 +112,7 @@
     E,
     PE,
     M,
+    PM,
     H,
     plane,
     depth,
@@ -132,15 +135,16 @@
     side_rad,
     side_spd,
     Gf,
-    env,
     in_sem,
-    out_sem,
     send_a,
     recv_a,
     send_b,
     recv_b,
     recv_r,
     send_r,
+    ready,
+    cross,
+    side,
 ):
     s = lax.axis_index("slab")
     t = lax.axis_index("tile")
@@ -155,12 +159,12 @@
     has_outer = (outer >= 0) & (outer < n_slab)
 
     def sender_of(q):
-        return jnp.where((col - q // NZ) % 2 == 0, q, col * NZ + q % NZ)
+        return col * NZ + q % NZ
 
     relayed = jnp.int32(0)
     is_relay = jnp.bool_(False)
     for i, q in enumerate(sources):
-        mine = (pos_z == q % NZ) & ((col - q // NZ) % 2 != 0)
+        mine = (pos_z == q % NZ) & ((col != q // NZ))
         relayed = jnp.where(mine, i, relayed)
         is_relay = is_relay | mine
 
@@ -192,36 +196,65 @@
     for c in loads:
         c.start()
 
+    late = pos_z >= EARLY
+    opens, closes = pos_z == 0, pos_z == NZ - 1
     bar = pltpu.get_barrier_semaphore()
     count = jnp.int32(0)
+    crossing = jnp.int32(0)
     for a, b in NEIGHBOURS:
         c = there(a, b)
-
-        @pl.when(c)
+        later = c & closes if b == 1 else jnp.bool_(False)
+        across = c & opens if b == -1 else jnp.bool_(False)
+
+        @pl.when(c & jnp.logical_not(later))
         def _():
             pl.semaphore_signal(bar, inc=1, device_id=(s + a, t + b), device_id_type=MESH)
 
-        count = count + c.astype(jnp.int32)
+        count = count + (c & jnp.logical_not(across)).astype(jnp.int32)
+        crossing = crossing + across.astype(jnp.int32)
+    outer_one = has_outer.astype(jnp.int32)
     for q in sources:
         sender = sender_of(q)
 
-        @pl.when(sender != t)
+        @pl.when((sender != t) & jnp.logical_not(late))
         def _():
             pl.semaphore_signal(bar, inc=1, device_id=(s, sender), device_id_type=MESH)
 
-        @pl.when(has_outer)
+        @pl.when(has_outer & jnp.logical_not(late))
         def _():
             pl.semaphore_signal(bar, inc=1, device_id=(outer, sender), device_id_type=MESH)
 
+        count = count + jnp.where(late, (t != sender).astype(jnp.int32) + outer_one, 0)
+
+    def greet_late(column):
+        for z in range(EARLY, NZ):
+            d = column * NZ + z
+
+            @pl.when(d != t)
+            def _():
+                pl.semaphore_signal(bar, inc=1, device_id=(s, d), device_id_type=MESH)
+
+            @pl.when(has_outer)
+            def _():
+                pl.semaphore_signal(bar, inc=1, device_id=(outer, d), device_id_type=MESH)
+
+    @pl.when(is_source)
+    def _():
+        greet_late(col)
+
     @pl.when(is_relay)
     def _():
+        greet_late(col)
+
+    @pl.when(is_relay)
+    def _():
         pl.semaphore_signal(bar, inc=1, device_id=(s, first + relayed), device_id_type=MESH)
 
-    half_tiles = n_tile // 2
-    count = count + jnp.where(
-        is_source, half_tiles - 1 + n_col // 2 + jnp.where(has_outer, half_tiles, 0), 0
-    )
-    count = count + jnp.where(is_relay, NZ - 1 + jnp.where(has_outer, NZ, 0), 0)
+    sends = jnp.where(is_source | is_relay, 1, 0)
+    me_late = late.astype(jnp.int32)
+    n_early = sends * EARLY * (1 + outer_one) - sends * (1 - me_late)
+    n_late = sends * (NZ - EARLY) * (1 + outer_one) - sends * me_late
+    count = count + n_early + jnp.where(is_source, n_col - 1, 0)
 
     @pl.when(s == 0)
     def _():
@@ -289,6 +322,61 @@
                 )
                 pk_out[d, 1] = jnp.where(left, jnp.where(odd, lo[3], lo[2]), far)
 
+    hi = lax.Precision.HIGHEST
+    pick_r = lax.broadcasted_iota(jnp.int32, (8, 128), 0)
+    lane48 = lanes(48)
+    wy = t * 64 + lane48 - jnp.where(lane48 < 100, 0, 128)
+    wx = lax.broadcasted_iota(jnp.int32, (48, 128), 0) + first * 8
+    def prepare():
+        for c in loads[1:]:
+            c.wait()
+        place = pos[...].reshape(1, 64)
+        value = ((seed[...].reshape(1, 64) & 63) + 1).astype(F32)
+        rows = lax.broadcasted_iota(jnp.int32, (512, 64), 0)
+        cells = lax.broadcasted_iota(jnp.int32, (128, 64), 0)
+        in_row = jnp.where(rows == (place >> 7), 1.0, 0.0).astype(jnp.bfloat16)
+        in_lane = jnp.where(cells == (place & 127), value, 0.0).astype(jnp.bfloat16)
+        named = lax.dot_general(
+            in_row, in_lane, (((1,), (1,)), ((), ())), preferred_element_type=F32
+        ).reshape(8, 64, 128)
+        theta = GOLDEN_ANGLE * lanes(8).astype(F32)
+        table = 1.0 + 0.5 * jnp.cos(4.0 * theta)
+        table = jnp.broadcast_to(table[0:1], (64, 128))
+        for z in range(8):
+            grain = jnp.where(named[z] > 0.5, named[z].astype(jnp.int32) - 1, lab[z] & 63)
+            spd[z] = lane_pick(table, grain)
+
+        nt = (((1,), (1,)), ((), ()))
+        e_rad = jnp.where(
+            ((pick_r == 0) & (lane8 == 127)) | ((pick_r == 2) & (lane8 == 0)), 1.0, 0.0
+        )
+        e_spd = jnp.where(
+            ((pick_r == 1) & (lane8 == 127)) | ((pick_r == 3) & (lane8 == 0)), 1.0, 0.0
+        )
+        cols[...] = lax.dot_general(
+            e_rad, rad[...].reshape(512, 128), nt, precision=hi, preferred_element_type=F32
+        ) + lax.dot_general(
+            e_spd, spd[...].reshape(512, 128), nt, precision=hi, preferred_element_type=F32
+        )
+
+        for step in range(2):
+            row = lax.broadcasted_iota(jnp.int32, (12, 16, 128), 0)
+            y = lax.broadcasted_iota(jnp.int32, (12, 16, 128), 1) * 128
+            y = y + lax.broadcasted_iota(jnp.int32, (12, 16, 128), 2)
+            xd = (t * 8 - 2 + row - spot[step, 0]).astype(F32)
+            yd = (y - spot[step, 1]).astype(F32)
+            plane[step] = SOURCE_POWER * jnp.exp(-(xd * xd + yd * yd) / BEAM_RADIUS_SQ)
+            xd = (wx - spot[step, 0]).astype(F32)
+            yd = (wy - spot[step, 1]).astype(F32)
+            side[step] = SOURCE_POWER * jnp.exp(-(xd * xd + yd * yd) / BEAM_RADIUS_SQ)
+        level = lax.broadcasted_iota(jnp.int32, (8, 16, 128), 0) + (s * 4 - 2)
+        depth[...] = jnp.exp(-(n_slab * 4 - 1 - level).astype(F32) / DEPTH_SCALE)
+
+
+    @pl.when(jnp.logical_not(late))
+    def _():
+        prepare()
+
     pl.semaphore_wait(bar, count)
 
     halos = []
@@ -313,11 +401,36 @@
                 ),
             )
         )
-    for a, b, copy in sorted(halos, key=lambda h: -h[1]):
-
-        @pl.when(there(a, b))
-        def _():
-            copy.start()
+    def now(a, b):
+        return there(a, b) & jnp.logical_not(opens) if b == -1 else there(a, b)
+
+    def send_halos():
+        for a, b, copy in sorted(halos, key=lambda h: -h[1]):
+
+            @pl.when(now(a, b))
+            def _():
+                copy.start()
+
+    for a in (-1, 0, 1):
+
+        @pl.when(there(a, 1) & closes)
+        def _():
+            pl.semaphore_signal(cross, inc=1, device_id=(s + a, t + 1), device_id_type=MESH)
+
+    @pl.when(jnp.logical_not(is_source))
+    def _():
+        send_halos()
+
+    for q in sources:
+        sender = sender_of(q)
+
+        @pl.when(late & (sender != t))
+        def _():
+            pl.semaphore_signal(ready, inc=1, device_id=(s, sender), device_id_type=MESH)
+
+        @pl.when(late & has_outer)
+        def _():
+            pl.semaphore_signal(ready, inc=1, device_id=(outer, sender), device_id_type=MESH)
 
     def send(kind, src, d, i):
         own = jnp.int32(i) if isinstance(i, int) else i
@@ -350,83 +463,43 @@
             device_id_type=MESH,
         )
 
+    own_slot = t - first
+
+    def relay_columns(z):
+        for c in (1, n_col - 1) + tuple(range(2, n_col - 1)):
+            d = (col + c) % n_col * NZ + z
+            at = (col + c) % n_col * NZ + pos_z
+            to_relay(0, d, at, z).start()
+
+            @pl.when(has_outer)
+            def _():
+                to_relay(1, d, at, z).start()
+
+    def direct_columns(z):
+        d = col * NZ + z
+
+        @pl.when(d != t)
+        def _():
+            send(0, pk_own.at[d], d, own_slot).start()
+
+        @pl.when(has_outer)
+        def _():
+            send(1, pk_out.at[d], d, own_slot).start()
+
     @pl.when(is_source)
     def _():
-        own = t - first
-
-        @pl.loop(0, NZ)
+        @pl.loop(0, FIRST)
         def _(z):
-            for c in range(0, n_col, 2):
-                d = (col + c + 1) % n_col * NZ + z
-                at = (col + c + 1) % n_col * NZ + pos_z
-                to_relay(0, d, at, z).start()
-
-                @pl.when(has_outer)
-                def _():
-                    to_relay(1, d, at, z).start()
-
-            for c in range(0, n_col, 2):
-                d = (col + c) % n_col * NZ + z
-
-                @pl.when(d != t)
-                def _():
-                    send(0, pk_own.at[d], d, own).start()
-
-                @pl.when(has_outer)
-                def _():
-                    send(1, pk_out.at[d], d, own).start()
-
-        in_own[own] = pk_own[t]
-
-    for c in loads[1:]:
-        c.wait()
-    place = pos[...].reshape(1, 64)
-    value = ((seed[...].reshape(1, 64) & 63) + 1).astype(F32)
-    rows = lax.broadcasted_iota(jnp.int32, (512, 64), 0)
-    cells = lax.broadcasted_iota(jnp.int32, (128, 64), 0)
-    in_row = jnp.where(rows == (place >> 7), 1.0, 0.0).astype(jnp.bfloat16)
-    in_lane = jnp.where(cells == (place & 127), value, 0.0).astype(jnp.bfloat16)
-    named = lax.dot_general(
-        in_row, in_lane, (((1,), (1,)), ((), ())), preferred_element_type=F32
-    ).reshape(8, 64, 128)
-    theta = GOLDEN_ANGLE * lanes(8).astype(F32)
-    table = 1.0 + 0.5 * jnp.cos(4.0 * theta)
-    table = jnp.broadcast_to(table[0:1], (64, 128))
-    for z in range(8):
-        grain = jnp.where(named[z] > 0.5, named[z].astype(jnp.int32) - 1, lab[z] & 63)
-        spd[z] = lane_pick(table, grain)
-
-    pick_r = lax.broadcasted_iota(jnp.int32, (8, 128), 0)
-    nt = (((1,), (1,)), ((), ()))
-    e_rad = jnp.where(
-        ((pick_r == 0) & (lane8 == 127)) | ((pick_r == 2) & (lane8 == 0)), 1.0, 0.0
-    )
-    e_spd = jnp.where(
-        ((pick_r == 1) & (lane8 == 127)) | ((pick_r == 3) & (lane8 == 0)), 1.0, 0.0
-    )
-    hi = lax.Precision.HIGHEST
-    cols[...] = lax.dot_general(
-        e_rad, rad[...].reshape(512, 128), nt, precision=hi, preferred_element_type=F32
-    ) + lax.dot_general(
-        e_spd, spd[...].reshape(512, 128), nt, precision=hi, preferred_element_type=F32
-    )
-
-    sides = []
-    lane48 = lanes(48)
-    wy = t * 64 + lane48 - jnp.where(lane48 < 100, 0, 128)
-    wx = lax.broadcasted_iota(jnp.int32, (48, 128), 0) + first * 8
-    for step in range(2):
-        row = lax.broadcasted_iota(jnp.int32, (12, 16, 128), 0)
-        y = lax.broadcasted_iota(jnp.int32, (12, 16, 128), 1) * 128
-        y = y + lax.broadcasted_iota(jnp.int32, (12, 16, 128), 2)
-        xd = (t * 8 - 2 + row - spot[step, 0]).astype(F32)
-        yd = (y - spot[step, 1]).astype(F32)
-        plane[step] = SOURCE_POWER * jnp.exp(-(xd * xd + yd * yd) / BEAM_RADIUS_SQ)
-        xd = (wx - spot[step, 0]).astype(F32)
-        yd = (wy - spot[step, 1]).astype(F32)
-        sides.append(SOURCE_POWER * jnp.exp(-(xd * xd + yd * yd) / BEAM_RADIUS_SQ))
-    level = lax.broadcasted_iota(jnp.int32, (8, 16, 128), 0) + (s * 4 - 2)
-    depth[...] = jnp.exp(-(n_slab * 4 - 1 - level).astype(F32) / DEPTH_SCALE)
+            relay_columns(z)
+            direct_columns(z)
+
+        send_halos()
+
+        in_own[own_slot] = pk_own[t]
+
+    @pl.when(late)
+    def _():
+        prepare()
 
     fine = []
     k0 = len(NEIGHBOURS)
@@ -454,68 +527,108 @@
     ]
     for a, b, copy in fine:
 
-        @pl.when(there(a, b))
+        @pl.when(now(a, b))
         def _():
             copy.start()
 
+    @pl.when(is_source)
+    def _():
+        @pl.loop(FIRST, EARLY)
+        def _(z):
+            relay_columns(z)
+            direct_columns(z)
+
+        @pl.loop(EARLY, NZ)
+        def _(z):
+            relay_columns(z)
+
+    def await_halos(before):
+        for a, b, copy in halos:
+            if (b == 1) == before:
+
+                @pl.when(there(-a, -b))
+                def _():
+                    copy.wait_recv()
+
+    def edges_of_step():
+        @pl.when(s == 0)
+        def _():
+            M[0:1] = jnp.zeros((1,) + M.shape[1:], F32)
+
+        @pl.when(s == n_slab - 1)
+        def _():
+            M[5:6] = jnp.zeros((1,) + M.shape[1:], F32)
+
+        @pl.when(t == 0)
+        def _():
+            M[:, 0:1] = jnp.zeros((6, 1) + M.shape[2:], F32)
+
+        @pl.when(t == n_tile - 1)
+        def _():
+            M[:, 9:10] = jnp.zeros((6, 1) + M.shape[2:], F32)
+
+    def first_part():
+        await_halos(False)
+        heat_step(E, PE, M, plane.at[0], depth.at[1:7], 8, 2, 10, 1, slice(2, 12), False)
+        edges_of_step()
+        heat_step(M, PM, H, plane.at[1], depth.at[2:6], 6, 2, 8, 2, slice(2, 10), False)
+
+    @pl.when(jnp.logical_not(late))
+    def _():
+        first_part()
+
+    def forward(z):
+        d = col * NZ + z
+        to_relay(0, d, t, z).wait_recv()
+
+        @pl.when(d != t)
+        def _():
+            send(0, rl_own.at[z], d, relayed).start()
+
+        @pl.when(d == t)
+        def _():
+            in_own[relayed] = rl_own[z]
+
+        @pl.when(has_outer)
+        def _():
+            to_relay(1, d, t, z).wait_recv()
+            send(1, rl_out.at[z], d, relayed).start()
+
     @pl.when(is_relay)
     def _():
-        @pl.loop(0, NZ)
+        @pl.loop(0, EARLY)
         def _(z):
-            d = col * NZ + z
-            to_relay(0, d, t, z).wait_recv()
-
-            @pl.when(d != t)
-            def _():
-                send(0, rl_own.at[z], d, relayed).start()
-
-            @pl.when(d == t)
-            def _():
-                in_own[relayed] = rl_own[z]
-
-            @pl.when(has_outer)
-            def _():
-                to_relay(1, d, t, z).wait_recv()
-                send(1, rl_out.at[z], d, relayed).start()
-
-    for a, b, copy in halos:
-
-        @pl.when(there(-a, -b))
-        def _():
-            copy.wait_recv()
-
-    for a, b, copy in halos:
-
-        @pl.when(there(a, b))
-        def _():
-            copy.wait_send()
-
-    heat_step(E, PE, M, plane.at[0], depth.at[1:7], 8, 12, 1)
-
-    @pl.when(s == 0)
-    def _():
-        M[0:1] = jnp.zeros((1,) + M.shape[1:], F32)
-
-    @pl.when(s == n_slab - 1)
-    def _():
-        M[5:6] = jnp.zeros((1,) + M.shape[1:], F32)
-
-    @pl.when(t == 0)
-    def _():
-        M[:, 0:1] = jnp.zeros((6, 1) + M.shape[2:], F32)
-
-    @pl.when(t == n_tile - 1)
-    def _():
-        M[:, 9:10] = jnp.zeros((6, 1) + M.shape[2:], F32)
-
-    heat_step(M, PE.at[0:6, 0:10], H, plane.at[1], depth.at[2:6], 6, 10, 2)
-
-    Hf = H.reshape(4 * 8 * 16, 128)
-    for z in range(4):
-        for k in range(16):
-            x_v[z, :, 128 * k : 128 * k + 128] = Hf[pl.ds(z * 128 + k, 8, stride=16), :]
-    heat_copy = pltpu.make_async_copy(x_v, heat_out, out_sem.at[0])
-    heat_copy.start()
+            forward(z)
+
+    @pl.when(opens & (t > 0))
+    def _():
+        pl.semaphore_wait(cross, crossing)
+        for a, b, copy in halos + fine:
+            if b == -1:
+
+                @pl.when(there(a, b))
+                def _():
+                    copy.start()
+
+    @pl.when(sends > 0)
+    def _():
+        pl.semaphore_wait(ready, n_late)
+
+    @pl.when(is_source)
+    def _():
+        @pl.loop(EARLY, NZ)
+        def _(z):
+            direct_columns(z)
+
+    @pl.when(is_relay)
+    def _():
+        @pl.loop(EARLY, NZ)
+        def _(z):
+            forward(z)
+
+    @pl.when(late)
+    def _():
+        first_part()
 
     for a, b, copy in fine:
 
@@ -545,6 +658,16 @@
         Gf[z, 0:8] = jnp.zeros((8, 128), F32)
         Gf[z, 72:80] = jnp.zeros((8, 128), F32)
 
+    await_halos(True)
+    heat_step(E, PE, M, plane.at[0], depth.at[1:7], 8, 0, 2, 1, slice(0, 2), True)
+    edges_of_step()
+    heat_step(M, PM, H, plane.at[1], depth.at[2:6], 6, 0, 2, 2, slice(0, 2), True)
+
+    Hf = H.reshape(4 * 8 * 16, 128)
+    for z in range(4):
+        for k in range(16):
+            heat_out[z, :, 128 * k : 128 * k + 128] = Hf[pl.ds(z * 128 + k, 8, stride=16), :]
+
     for i, q in enumerate(sources):
 
         @pl.when(sender_of(q) != t)
@@ -592,7 +715,7 @@
                 put(i, 7 + z, in_sib[i, z % 2], z >= 2, in_sib[i, 2], 6 * z)
 
     keep = (lane48 < 64) | ((lane48 < 100) & (t < n_tile - 1)) | ((lane48 >= 100) & (t > 0))
-    window_step(V, PV, VM, sides[0], depth, 10, keep)
+    window_step(V, PV, VM, side[0], depth, 10, keep)
 
     @pl.when(s == 0)
     def _():
@@ -602,7 +725,7 @@
     def _():
         VM[6:8] = jnp.zeros((2,) + VM.shape[1:], F32)
 
-    window_step(VM, PV.at[0:8], VH, sides[1], depth.at[1:7], 8, keep)
+    window_step(VM, PV.at[0:8], VH, side[1], depth.at[1:7], 8, keep)
 
     @pl.when(s == 0)
     def _():
@@ -655,9 +778,12 @@
         )
         near_x = jnp.maximum(Gf[zf + 1, 7:71], Gf[zf + 1, 9:73])
         near_z = jnp.maximum(Gf[zf, 8:72], Gf[zf + 2, 8:72])
-        env[zf] = jnp.maximum(c, jnp.maximum(jnp.maximum(near_x, near_y), near_z) - 0.5)
-    env_copy = pltpu.make_async_copy(env, grown_out, out_sem.at[1])
-    env_copy.start()
+        grown_out[zf] = jnp.maximum(c, jnp.maximum(jnp.maximum(near_x, near_y), near_z) - 0.5)
+    for a, b, copy in halos:
+
+        @pl.when(there(a, b))
+        def _():
+            copy.wait_send()
 
     for i in range(6):
         to_sibling(i).wait_send()
@@ -674,9 +800,6 @@
         @pl.loop(0, n_out)
         def _(d):
             send(1, pk_out.at[0], t, 0).wait_send()
-
-    heat_copy.wait()
-    env_copy.wait()
 
 
 def local(temperature, spot, labels, radius, position, seeds):
@@ -688,11 +811,11 @@
     return pl.pallas_call(
         body,
         out_shape=(
-            jax.ShapeDtypeStruct((4, 8, 2048), F32),
-            jax.ShapeDtypeStruct((8, 64, 128), F32),
+            vm((4, 8, 2048), F32),
+            vm((8, 64, 128), F32),
         ),
         in_specs=[any_spec] * 6,
-        out_specs=(any_spec, any_spec),
+        out_specs=(pl.BlockSpec(memory_space=pltpu.VMEM),) * 2,
         scratch_shapes=[
             vm((4, 8, 2048), F32),
             pltpu.SMEM((2, 2), jnp.int32),
@@ -703,6 +826,7 @@
             vm((8, 64, 128), F32),
             vm((8, 12, 16, 128), F32),
             vm((8, 12, 16, 128), F32),
+            vm((6, 10, 16, 128), F32),
             vm((6, 10, 16, 128), F32),
             vm((4, 8, 16, 128), F32),
             vm((2, 12, 16, 128), F32),
@@ -726,15 +850,16 @@
             vm((8, 64, 128), F32),
             vm((8, 64, 128), F32),
             vm((10, 80, 128), F32),
-            vm((8, 64, 128), F32),
             dma((6,)),
-            dma((2,)),
             dma((14,)),
             dma((14,)),
             dma((2,)),
             dma((3, 6)),
             dma((2, NZ)),
             dma((1,)),
+            pltpu.SemaphoreType.REGULAR,
+            pltpu.SemaphoreType.REGULAR,
+            vm((2, 48, 128), F32),
         ],
         compiler_params=pltpu.CompilerParams(collective_id=0, has_side_effects=True),
         name="build_step",

time: 29.6 us -> 26.7 us (0.902)
  the two profiles are of different devices: /device:TPU:94 before, /device:TPU:17 now
where the time goes in v3:
time: 26.7 us; the launch traced here: 26.5 us
  Pallas kernels  24.5 us (92%)
  local copies, waits for them, and re-layouts  1.41 us (5%)
  between operations  0.64 us (2%)
    pallas_call x1, Pallas kernels, local(): pl.pallas_call(body, out_shape=(vm((4, 8, 2048), F32), vm((8, 64, 128), F...  24.5 us
    unnamed x2, local copies, waits for them, and re-layouts  1.41 us

profile of v3, /device:TPU:17, one launch (start us, length us, event | category | flops | bytes accessed | tf_op | source)
XLA Modules:
  0.0 26.5 jit_solution(8528135543024370389)
XLA Ops:
  0.6 24.5 %build_step.1 = (f32[4,8,2048]{2,1,0:T(8,128)S(1)}, f32[8,64,128]{2,1,0:T(8,128)S(1)}) custom-call(f32[4,8,2048]{2,1,0:T(8,128)} %refs_0_.1, s32[2,2]{1,0:T(2,128)} %refs_1_.1, s32[8,64,128]{2,1,0:T(8,128)} %refs_2_.1, f32[8,64,128]{2,1,0:T(8,128)} %refs_3_.1, s32[64]{0:T(128)} %refs_4_.1, s32[64]{0:T(128)} %refs_5_.1), custom_call_target="tpu_custom_call" | custom-call | tf_op jit(solution)/shard_map/build_step/pallas_call | solution.py:811
  25.1 0.7 %copy.10 = f32[4,8,2048]{2,1,0:T(8,128)} copy(f32[4,8,2048]{2,1,0:T(8,128)S(1)} %get-tuple-element.2) | data formatting | bytes 524288
  25.8 0.7 %copy.11 = f32[8,64,128]{2,1,0:T(8,128)} copy(f32[8,64,128]{2,1,0:T(8,128)S(1)} %get-tuple-element.3) | data formatting | bytes 524288

commit v4 on v3

--- a/solution.py
+++ b/solution.py
@@ -180,6 +180,28 @@
             c = c & (t < n_tile - 1)
         return c
 
+    bar = pltpu.get_barrier_semaphore()
+
+    @pl.when(is_relay)
+    def _():
+        pl.semaphore_signal(bar, inc=1, device_id=(s, first + relayed), device_id_type=MESH)
+
+    outer_one = has_outer.astype(jnp.int32)
+
+    @pl.when(is_source | is_relay)
+    def _():
+        for z in range(EARLY, NZ):
+            d = col * NZ + z
+            apart = jnp.abs(pos_z - z) > 1
+
+            @pl.when(apart)
+            def _():
+                pl.semaphore_signal(bar, inc=1, device_id=(s, d), device_id_type=MESH)
+
+            @pl.when(apart & has_outer)
+            def _():
+                pl.semaphore_signal(bar, inc=1, device_id=(outer, d), device_id_type=MESH)
+
     loads = [
         pltpu.make_async_copy(a, b, in_sem.at[i])
         for i, (a, b) in enumerate(
@@ -198,7 +220,6 @@
 
     late = pos_z >= EARLY
     opens, closes = pos_z == 0, pos_z == NZ - 1
-    bar = pltpu.get_barrier_semaphore()
     count = jnp.int32(0)
     crossing = jnp.int32(0)
     for a, b in NEIGHBOURS:
@@ -212,7 +233,6 @@
 
         count = count + (c & jnp.logical_not(across)).astype(jnp.int32)
         crossing = crossing + across.astype(jnp.int32)
-    outer_one = has_outer.astype(jnp.int32)
     for q in sources:
         sender = sender_of(q)
 
@@ -224,31 +244,8 @@
         def _():
             pl.semaphore_signal(bar, inc=1, device_id=(outer, sender), device_id_type=MESH)
 
-        count = count + jnp.where(late, (t != sender).astype(jnp.int32) + outer_one, 0)
-
-    def greet_late(column):
-        for z in range(EARLY, NZ):
-            d = column * NZ + z
-
-            @pl.when(d != t)
-            def _():
-                pl.semaphore_signal(bar, inc=1, device_id=(s, d), device_id_type=MESH)
-
-            @pl.when(has_outer)
-            def _():
-                pl.semaphore_signal(bar, inc=1, device_id=(outer, d), device_id_type=MESH)
-
-    @pl.when(is_source)
-    def _():
-        greet_late(col)
-
-    @pl.when(is_relay)
-    def _():
-        greet_late(col)
-
-    @pl.when(is_relay)
-    def _():
-        pl.semaphore_signal(bar, inc=1, device_id=(s, first + relayed), device_id_type=MESH)
+        apart = jnp.abs(pos_z - q % NZ) > 1
+        count = count + jnp.where(late & apart, 1 + outer_one, 0)
 
     sends = jnp.where(is_source | is_relay, 1, 0)
     me_late = late.astype(jnp.int32)
@@ -359,6 +356,7 @@
             e_spd, spd[...].reshape(512, 128), nt, precision=hi, preferred_element_type=F32
         )
 
+    def prepare_beam():
         for step in range(2):
             row = lax.broadcasted_iota(jnp.int32, (12, 16, 128), 0)
             y = lax.broadcasted_iota(jnp.int32, (12, 16, 128), 1) * 128
@@ -376,6 +374,7 @@
     @pl.when(jnp.logical_not(late))
     def _():
         prepare()
+        prepare_beam()
 
     pl.semaphore_wait(bar, count)
 
@@ -465,8 +464,8 @@
 
     own_slot = t - first
 
-    def relay_columns(z):
-        for c in (1, n_col - 1) + tuple(range(2, n_col - 1)):
+    def relay_columns(z, columns):
+        for c in columns:
             d = (col + c) % n_col * NZ + z
             at = (col + c) % n_col * NZ + pos_z
             to_relay(0, d, at, z).start()
@@ -490,7 +489,7 @@
     def _():
         @pl.loop(0, FIRST)
         def _(z):
-            relay_columns(z)
+            relay_columns(z, (n_col // 2, 1, n_col - 1))
             direct_columns(z)
 
         send_halos()
@@ -535,12 +534,43 @@
     def _():
         @pl.loop(FIRST, EARLY)
         def _(z):
-            relay_columns(z)
+            relay_columns(z, (n_col // 2, 1, n_col - 1))
             direct_columns(z)
 
         @pl.loop(EARLY, NZ)
         def _(z):
-            relay_columns(z)
+            relay_columns(z, (n_col // 2,))
+
+        @pl.loop(EARLY, NZ)
+        def _(z):
+            relay_columns(z, (1, n_col - 1))
+
+    def forward(z):
+        d = col * NZ + z
+        to_relay(0, d, t, z).wait_recv()
+
+        @pl.when(d != t)
+        def _():
+            send(0, rl_own.at[z], d, relayed).start()
+
+        @pl.when(d == t)
+        def _():
+            in_own[relayed] = rl_own[z]
+
+        @pl.when(has_outer)
+        def _():
+            to_relay(1, d, t, z).wait_recv()
+            send(1, rl_out.at[z], d, relayed).start()
+
+    @pl.when(is_relay)
+    def _():
+        @pl.loop(0, EARLY)
+        def _(z):
+            forward(z)
+
+    @pl.when(late)
+    def _():
+        prepare_beam()
 
     def await_halos(before):
         for a, b, copy in halos:
@@ -577,29 +607,6 @@
     def _():
         first_part()
 
-    def forward(z):
-        d = col * NZ + z
-        to_relay(0, d, t, z).wait_recv()
-
-        @pl.when(d != t)
-        def _():
-            send(0, rl_own.at[z], d, relayed).start()
-
-        @pl.when(d == t)
-        def _():
-            in_own[relayed] = rl_own[z]
-
-        @pl.when(has_outer)
-        def _():
-            to_relay(1, d, t, z).wait_recv()
-            send(1, rl_out.at[z], d, relayed).start()
-
-    @pl.when(is_relay)
-    def _():
-        @pl.loop(0, EARLY)
-        def _(z):
-            forward(z)
-
     @pl.when(opens & (t > 0))
     def _():
         pl.semaphore_wait(cross, crossing)
@@ -610,25 +617,37 @@
                 def _():
                     copy.start()
 
-    @pl.when(sends > 0)
-    def _():
-        pl.semaphore_wait(ready, n_late)
-
-    @pl.when(is_source)
-    def _():
-        @pl.loop(EARLY, NZ)
-        def _(z):
-            direct_columns(z)
-
-    @pl.when(is_relay)
-    def _():
-        @pl.loop(EARLY, NZ)
-        def _(z):
-            forward(z)
+    def late_sends():
+        @pl.when(sends > 0)
+        def _():
+            pl.semaphore_wait(ready, n_late)
+
+        @pl.when(is_source)
+        def _():
+            @pl.loop(EARLY, NZ)
+            def _(z):
+                direct_columns(z)
+
+        @pl.when(is_relay)
+        def _():
+            @pl.loop(EARLY, NZ)
+            def _(z):
+                forward(z)
+
+    late_sends()
 
     @pl.when(late)
     def _():
         first_part()
+
+    order = (5, 4, 3, 2, 1, 0)
+    for i in order:
+
+        @pl.when(sender_of(sources[i]) != t)
+        def _():
+            send(0, pk_own.at[0], t, i).wait_recv()
+
+        to_sibling(i).start()
 
     for a, b, copy in fine:
 
@@ -668,18 +687,6 @@
         for k in range(16):
             heat_out[z, :, 128 * k : 128 * k + 128] = Hf[pl.ds(z * 128 + k, 8, stride=16), :]
 
-    for i, q in enumerate(sources):
-
-        @pl.when(sender_of(q) != t)
-        def _():
-            send(0, pk_own.at[0], t, i).wait_recv()
-
-        to_sibling(i).start()
-
-        @pl.when(has_outer)
-        def _():
-            send(1, pk_out.at[0], t, i).wait_recv()
-
     far_lane = jnp.where(lane8 >= 100, lane8 - 125, lane8 - 61)
 
     def put(i, z, tile, high, halo, base):
@@ -687,32 +694,39 @@
         around = lane_pick(halo, (far_lane + base) & 127)
         V[z, 8 + 8 * i : 16 + 8 * i] = jnp.where(left, body, around)
 
-    for i in range(6):
+    def own_layers(i):
         for z in range(4):
             put(i, 3 + z, in_own[i, z % 2], z >= 2, in_own[i, 2], 6 * z)
 
-    @pl.when(has_outer)
-    def _():
-        at = jnp.where(odd, 7, 0)
-        base = 64 + jnp.where(odd, 0, 6)
-        for i in range(6):
+    def outer_layers(group):
+        @pl.when(has_outer)
+        def _():
+            for i in group:
+                send(1, pk_out.at[0], t, i).wait_recv()
+            at = jnp.where(odd, 7, 0)
+            base = 64 + jnp.where(odd, 0, 6)
+            for i in group:
+                for z in range(3):
+                    put(i, at + z, in_out[i, z // 2], z == 1, in_out[i, 1], base + 6 * z)
+
+    def sibling_layers(group):
+        for i in group:
+            to_sibling(i).wait_recv()
+        at = jnp.where(odd, 0, 7)
+        skip = odd.astype(jnp.int32)
+        for i in group:
+            halo = in_sib[i, 2]
             for z in range(3):
-                put(i, at + z, in_out[i, z // 2], z == 1, in_out[i, 1], base + 6 * z)
-
-    for i in range(6):
-        to_sibling(i).wait_recv()
-
-    @pl.when(odd)
-    def _():
-        for i in range(6):
-            for z in range(3):
-                put(i, z, in_sib[i, (z + 1) % 2], z >= 1, in_sib[i, 2], 6 * (z + 1))
-
-    @pl.when(jnp.logical_not(odd))
-    def _():
-        for i in range(6):
-            for z in range(3):
-                put(i, 7 + z, in_sib[i, z % 2], z >= 2, in_sib[i, 2], 6 * z)
+                tile = in_sib[i, (z + skip) % 2]
+                body = jnp.where(z + skip >= 2, pltpu.roll(tile, 64, 1), tile)
+                around = lane_pick(halo, (far_lane + 6 * (z + skip)) & 127)
+                V[at + z, 8 + 8 * i : 16 + 8 * i] = jnp.where(left, body, around)
+
+    for group in (order,):
+        for i in group:
+            own_layers(i)
+        outer_layers(group)
+        sibling_layers(group)
 
     keep = (lane48 < 64) | ((lane48 < 100) & (t < n_tile - 1)) | ((lane48 >= 100) & (t > 0))
     window_step(V, PV, VM, side[0], depth, 10, keep)

time: 26.7 us -> 26 us (0.974)
  the two profiles are of different devices: /device:TPU:17 before, /device:TPU:23 now
where the time goes in v4:
time: 26 us; the launch traced here: 25.8 us
  Pallas kernels  23.7 us (91%)
  local copies, waits for them, and re-layouts  1.41 us (5%)
  between operations  0.64 us (2%)
    pallas_call x1, Pallas kernels, local(): pl.pallas_call(body, out_shape=(vm((4, 8, 2048), F32), vm((8, 64, 128), F...  23.7 us
    unnamed x2, local copies, waits for them, and re-layouts  1.41 us

profile of v4, /device:TPU:23, one launch (start us, length us, event | category | flops | bytes accessed | tf_op | source)
XLA Modules:
  0.0 25.8 jit_solution(1858488740550797957)
XLA Ops:
  0.6 23.7 %build_step.1 = (f32[4,8,2048]{2,1,0:T(8,128)S(1)}, f32[8,64,128]{2,1,0:T(8,128)S(1)}) custom-call(f32[4,8,2048]{2,1,0:T(8,128)} %refs_0_.1, s32[2,2]{1,0:T(2,128)} %refs_1_.1, s32[8,64,128]{2,1,0:T(8,128)} %refs_2_.1, f32[8,64,128]{2,1,0:T(8,128)} %refs_3_.1, s32[64]{0:T(128)} %refs_4_.1, s32[64]{0:T(128)} %refs_5_.1), custom_call_target="tpu_custom_call" | custom-call | tf_op jit(solution)/shard_map/build_step/pallas_call | solution.py:825
  24.4 0.7 %copy.10 = f32[4,8,2048]{2,1,0:T(8,128)} copy(f32[4,8,2048]{2,1,0:T(8,128)S(1)} %get-tuple-element.2) | data formatting | bytes 524288
  25.1 0.7 %copy.11 = f32[8,64,128]{2,1,0:T(8,128)} copy(f32[8,64,128]{2,1,0:T(8,128)S(1)} %get-tuple-element.3) | data formatting | bytes 524288

commit v5 on v4

--- a/solution.py
+++ b/solution.py
@@ -404,7 +404,7 @@
         return there(a, b) & jnp.logical_not(opens) if b == -1 else there(a, b)
 
     def send_halos():
-        for a, b, copy in sorted(halos, key=lambda h: -h[1]):
+        for a, b, copy in sorted(halos, key=lambda h: (-h[1], abs(h[0]))):
 
             @pl.when(now(a, b))
             def _():

time: 26 us -> 26 us (level)
  no operation moved by 1% of the time
where the time goes in v5:
time: 26 us; the launch traced here: 25.9 us
  Pallas kernels  23.8 us (92%)
  local copies, waits for them, and re-layouts  1.41 us (5%)
  between operations  0.64 us (2%)
    pallas_call x1, Pallas kernels, local(): pl.pallas_call(body, out_shape=(vm((4, 8, 2048), F32), vm((8, 64, 128), F...  23.8 us
    unnamed x2, local copies, waits for them, and re-layouts  1.41 us

profile of v5, /device:TPU:23, one launch (start us, length us, event | category | flops | bytes accessed | tf_op | source)
XLA Modules:
  0.0 25.9 jit_solution(11407792061944792567)
XLA Ops:
  0.6 23.8 %build_step.1 = (f32[4,8,2048]{2,1,0:T(8,128)S(1)}, f32[8,64,128]{2,1,0:T(8,128)S(1)}) custom-call(f32[4,8,2048]{2,1,0:T(8,128)} %refs_0_.1, s32[2,2]{1,0:T(2,128)} %refs_1_.1, s32[8,64,128]{2,1,0:T(8,128)} %refs_2_.1, f32[8,64,128]{2,1,0:T(8,128)} %refs_3_.1, s32[64]{0:T(128)} %refs_4_.1, s32[64]{0:T(128)} %refs_5_.1), custom_call_target="tpu_custom_call" | custom-call | tf_op jit(solution)/shard_map/build_step/pallas_call | solution.py:825
  24.5 0.7 %copy.10 = f32[4,8,2048]{2,1,0:T(8,128)} copy(f32[4,8,2048]{2,1,0:T(8,128)S(1)} %get-tuple-element.2) | data formatting | bytes 524288
  25.2 0.7 %copy.11 = f32[8,64,128]{2,1,0:T(8,128)} copy(f32[8,64,128]{2,1,0:T(8,128)S(1)} %get-tuple-element.3) | data formatting | bytes 524288
